TPU v7x, 256 devices: a whole 4x4x8 slice. The times are simulated.
256 devices in a mesh: row: 8 (over z_lo, y), col: 32 (over z_hi, x, core).
Axes of the slice: x: 4, y: 4, z: 8 (z_hi: 4, z_lo: 2; z = z_hi * 2 + z_lo), core: 2. Of those that a mesh axis runs over, the one named last changes fastest.
Arguments:
- points: float32 [16, 32768], P(None, ('row', 'col')), may hold values from -6 to 6
- inverse_length: float32 [16], replicated, may hold values from 0.35 to 1.4
- target: float32 [32768], P(('row', 'col')), may hold values from -6 to 6
- probe_bits: int32 [15, 32768], P(None, ('row', 'col')), may hold values from 0 to 1
- leaf_inverse: float32 [32768, 128], P(('row', 'col')), may hold values from -1 to 4, as said below
- top_basis: float32 [64, 32768], P(None, ('row', 'col')), may hold values from -0.09375 to 0.09375
- sub_basis: float32 [64, 32768], P(None, ('row', 'col')), may hold values from -0.1875 to 0.1875
Outputs:
- solution: float32 [16, 32768], P(None, ('row', 'col'))
- residual: float32 [16, 32768], P(None, ('row', 'col'))
- coefficients: float32 [2, 2, 16], replicated
Inputs may be any that keep to these rules, and one draw needn't show every extreme that they name: `leaf_inverse`: each leaf block is symmetric, and each of its diagonal entries exceeds the sum of the absolute values of the other entries of its row.
All inputs are finite; a program needn't handle non-finite values.
Results may differ from a plain program's by a relative error of at most 0.0003.
Values sent between devices are 32-bit elements; how exact they have to be, the bound alone decides.
No kernel may reach another device: no remote copies, remote signals or barrier semaphores. Data moves between devices by JAX's collectives and lax.ppermute only.
A program may use at most 64 MiB of HBM per device.

v0:
```python
import functools
import math

import jax
import jax.numpy as jnp
from jax import lax
from jax.experimental import pallas as pl
from jax.experimental.pallas import tpu as pltpu
from jax.sharding import Mesh
from jax.sharding import PartitionSpec as P

AXES = ("zl", "y", "zh", "x", "c")
GA = ("y", "x")
GB = ("zl", "zh", "c")
NG = 16
NT = 8
COLS = 16
PTS = 128
RANK = 64
NOISE = 0.5
F32 = jnp.float32
BF16 = jnp.bfloat16
LN2 = math.log(2.0)
COORD_SCALE = math.sqrt(5.0) / LN2
LEAD = LN2 * LN2 / 3.0
SHIFT = 1.5 / LN2
REST = 1.0 / LEAD - SHIFT * SHIFT
HIGHEST = lax.Precision.HIGHEST


def dot_nt(a, b):
    return lax.dot_general(a, b, (((1,), (1,)), ((), ())), precision=HIGHEST, preferred_element_type=F32)


def dot_nn(a, b):
    return lax.dot_general(a, b, (((1,), (0,)), ((), ())), precision=HIGHEST, preferred_element_type=F32)


def lane(shape):
    return lax.broadcasted_iota(jnp.int32, shape, 1)


def sublane(shape):
    return lax.broadcasted_iota(jnp.int32, shape, 0)


def pack(sums):
    shape = (COLS, PTS)
    acc = jnp.zeros(shape, F32)
    for k, s in enumerate(sums):
        acc = jnp.where(lane(shape) == COLS * k + sublane(shape), jnp.broadcast_to(s, shape), acc)
    return jnp.sum(acc, 0, keepdims=True)


def unpack(row, k):
    shape = (COLS, PTS)
    hit = lane(shape) == COLS * k + sublane(shape)
    return jnp.sum(jnp.where(hit, jnp.broadcast_to(row, shape), 0.0), 1, keepdims=True)


def rowdot(a, b):
    return jnp.sum(a * b, 1, keepdims=True)


def tile_rows(rows):
    shape = (8, PTS)
    out = jnp.zeros(shape, F32)
    for k, r in enumerate(rows):
        out = jnp.where(sublane(shape) == k, jnp.broadcast_to(r, shape), out)
    return out


def tree_sum(terms):
    terms = list(terms)
    while len(terms) > 1:
        terms = [terms[i] + terms[i + 1] if i + 1 < len(terms) else terms[i] for i in range(0, len(terms), 2)]
    return terms[0]


VMEM = pltpu.MemorySpace.VMEM
SMEM = pltpu.MemorySpace.SMEM
HBM = pltpu.MemorySpace.HBM


def call(kernel, outs, *args, spaces=None, out_spaces=None, limit=8 << 20, scratch=(), name=None):
    spaces = spaces or [VMEM] * len(args)
    out_spaces = out_spaces or [VMEM] * len(outs)
    args = [pltpu.with_memory_space_constraint(a, m) if m is HBM else a for a, m in zip(args, spaces)]
    return pl.pallas_call(
        kernel,
        out_shape=[m(s, d) if m is HBM else jax.ShapeDtypeStruct(s, d) for m, (s, d) in zip(out_spaces, outs)],
        in_specs=[pl.BlockSpec(memory_space=m) for m in spaces],
        out_specs=[pl.BlockSpec(memory_space=m) for m in out_spaces],
        scratch_shapes=list(scratch),
        compiler_params=pltpu.CompilerParams(vmem_limit_bytes=limit),
        name=name,
    )(*args)


SEND0 = 12 * COLS
BASES = slice(3 * COLS, 3 * COLS + PTS)
LEAF_PART = slice(11 * COLS, 12 * COLS)


def start_kernel(where, inv_h, points_h, target_h, bits_h, top_h, sub_h, leaf_h, send, rhs, basis, leaf, leaf_part, marks, points, target, bits, inv, sems):
    moves = [
        pltpu.make_async_copy(src, dst, sems.at[k])
        for k, (src, dst) in enumerate(
            [
                (bits_h, bits),
                (target_h, target),
                (top_h, basis.at[pl.ds(0, RANK)]),
                (sub_h, basis.at[pl.ds(RANK, RANK)]),
                (points_h, points),
                (inv_h, inv),
                (leaf_h, leaf),
            ]
        )
    ]
    for m in moves:
        m.start()
    row = sublane((NG + 8, PTS))
    place = where[0]
    hit = (row == lax.rem(place, NG)) | ((row >= NG) & (place >= NG))
    marks[...] = jnp.where(hit, 1.0, 0.0)
    for m in moves:
        m.wait()
    scale = jnp.zeros((COLS, PTS), F32)
    for k in range(COLS):
        scale = jnp.where(sublane((COLS, PTS)) == k, inv[k], scale)
    rhs[0:1, :] = target[...]
    rhs[1:COLS, :] = 2.0 * bits[...].astype(F32) - 1.0
    send[0:COLS, :] = points[...] * scale
    send[COLS : 2 * COLS, :] = dot_nt(rhs[...], basis[...])
    leaf_part[...] = dot_nt(rhs[...], leaf[...])


def fold_tiles(got, first, scalars, send, at):
    low = lane((COLS, PTS)) < RANK
    zero = tree_sum([got[j, first : first + COLS] for j in range(NG // 2)])
    one = tree_sum([got[j, first : first + COLS] for j in range(NG // 2, NG)])
    send[at : at + COLS, :] = jnp.where(low, zero + one, zero)
    send[at + COLS : at + 2 * COLS, :] = jnp.where(low, 0.0, one)
    if scalars:
        own = tree_sum([got[j, scalars : scalars + 8] for j in range(NG)])
        send[at + COLS : at + COLS + 8, :] = jnp.where(low[0:8], own, one[0:8])


def fold0_kernel(got, own, basis, leaf_part, send):
    send[0:COLS, :] = own[0:COLS, :]
    fold_tiles(got, COLS, 0, send, COLS)
    send[BASES, :] = basis[...]
    send[LEAF_PART, :] = leaf_part[...]


def fold1_kernel(got, leaf_part, send):
    fold_tiles(got, 0, COLS, send, 0)
    send[2 * COLS : 3 * COLS, :] = leaf_part[...]


def fold2_kernel(got, send):
    fold_tiles(got, 0, COLS, send, 0)


def sum_tiles(got, first):
    return [
        tree_sum([got[4 * y + x, at : at + COLS] for x in range(4)]) for at in (first, first + COLS) for y in range(4)
    ]


def column_directions(marks, table, leaf_parts, got0, directions):
    low = lane((COLS, PTS)) < RANK
    odd = marks[NG : NG + 1, :] > 0.5
    top = tree_sum(table[0:4])
    for y in range(4):
        coefs = jnp.where(low, top, jnp.where(odd, table[4 + y], table[y]))
        high = coefs.astype(BF16)
        both = jnp.concatenate([high, (coefs - high.astype(F32)).astype(BF16)], 0)
        for j in range(4 * y, 4 * y + 4):
            bases = got0[j, BASES]
            first = bases.astype(BF16)
            r = jnp.dot(both, first, preferred_element_type=F32)
            r = r[0:COLS] + r[COLS:] + jnp.dot(high, (bases - first.astype(F32)).astype(BF16), preferred_element_type=F32)
            directions[j] = leaf_parts(j) + r


def own_direction(marks, directions):
    return tree_sum([directions[j] * marks[j : j + 1, :] for j in range(NG)])


def features(x, left):
    def pieces(v):
        first = v.astype(BF16).astype(F32)
        second = (v - first).astype(BF16).astype(F32)
        third = (v - first - second).astype(BF16).astype(F32)
        return first, second, third

    a, b, c = pieces(x)
    norms = pieces(jnp.sum(x * x, 0, keepdims=True))
    ones = (jnp.ones((1, PTS), F32),) * 3
    if left:
        parts = [a, a, b, b, a, c]
        tail = tile_rows(norms + ones)
    else:
        a, b, c = -2.0 * a, -2.0 * b, -2.0 * c
        parts = [a, b, a, b, c, a]
        tail = tile_rows(ones + norms)
    return jnp.concatenate(parts + [tail, jnp.zeros((PTS - 6 * COLS - 8, PTS), F32)], 0)


def matern_kernel(left, right, high, low, left_f, right_f):
    for j in range(NG):
        at = slice(j * PTS, (j + 1) * PTS)
        right_f[:, at] = features(right[j, 0:COLS] * COORD_SCALE, False).astype(BF16)
        left_f[at, :] = features(left[j, 0:COLS] * COORD_SCALE, True).T.astype(BF16)
    height, width = 1024, 256

    def step(i, carry):
        rows = pl.ds(pl.multiple_of(i * height, height), height)
        lhs = left_f[rows, :]
        for j in range(0, NG * PTS, width):
            s = jnp.dot(lhs, right_f[:, j : j + width], preferred_element_type=F32)
            s = jnp.maximum(s, 1e-30)
            v = s * lax.rsqrt(s)
            w = v + SHIFT
            k = (w * w + REST) * jnp.exp2(-v)
            h = k.astype(BF16)
            high[rows, j : j + width] = h
            low[rows, j : j + width] = (k - h.astype(F32)).astype(BF16)
        return carry

    lax.fori_loop(0, NG * PTS // height, step, 0)


def matvec(directions, high, low, out):
    v = jnp.concatenate([directions[j] * LEAD for j in range(NG)], 1)
    v_high = v.astype(BF16)
    both = jnp.concatenate([v_high, (v - v_high.astype(F32)).astype(BF16)], 0)
    width = 512
    for j in range(0, NG * PTS, width):
        r = jnp.dot(both, high[:, j : j + width], preferred_element_type=F32)
        r = r[0:COLS] + r[COLS:] + jnp.dot(v_high, low[:, j : j + width], preferred_element_type=F32)
        for b in range(width // PTS):
            out[j // PTS + b] = r[:, b * PTS : (b + 1) * PTS]


def first_kernel(marks, got_a, high, low, out, z, table, directions):
    now = sum_tiles(got_a, COLS)
    for t in range(NT):
        table[t] = now[t]
    column_directions(marks, now, lambda j: got_a[j, LEAF_PART], got_a, directions)
    z[...] = own_direction(marks, directions)
    matvec(directions, high, low, out)


def image0_kernel(got, z, rhs, basis, leaf, q, leaf_part, send):
    q[...] = tree_sum([got[j] for j in range(NG)]) + NOISE * z[...]
    send[0:COLS, :] = dot_nt(q[...], basis[...])
    send[COLS:, :] = tile_rows([pack([rowdot(rhs[...], z[...]), rowdot(z[...], q[...])])])
    leaf_part[...] = dot_nt(q[...], leaf[...])


def second_kernel(marks, got, got0, table0, rhs, q, high, low, out, z, res, table, table_q, sums, directions):
    now = sum_tiles(got, 0)
    total = tree_sum(now[4:8])
    sums[...] = total[0:8]
    alpha = unpack(total[0:1], 0) / unpack(total[0:1], 1)
    for t in range(NT):
        table_q[t] = now[t]
        now[t] = table0[t] - alpha * now[t]
        table[t] = now[t]
    column_directions(
        marks, now, lambda j: got0[j, LEAF_PART] - alpha * got[j, 2 * COLS : 3 * COLS], got0, directions
    )
    z[...] = own_direction(marks, directions)
    res[...] = rhs[...] - alpha * q[...]
    matvec(directions, high, low, out)


def image1_kernel(got, z1, z0, res, q, leaf, basis, p, send):
    p[...] = tree_sum([got[j] for j in range(NG)]) + NOISE * z1[...]
    send[0:COLS, :] = dot_nt(p[...], basis[...])
    rv, qv, pv, zv = res[...], q[...], p[...], z1[...]
    rb, qb, pb = (dot_nt(v, leaf[...]) for v in (rv, qv, pv))
    rows = [
        pack([rowdot(rv, zv), rowdot(zv, pv), rowdot(zv, qv), rowdot(z0[...], pv)]),
        pack([rowdot(rv, rb), rowdot(rv, qb), rowdot(rv, pb)]),
        pack([rowdot(qv, qb), rowdot(qv, pb), rowdot(pv, pb)]),
    ]
    send[COLS:, :] = tile_rows(rows)


def finish_kernel(got, z0, z1, res, q, p, table1, table_q, sums0, x_out, r_out, coefs):
    now = sum_tiles(got, 0)
    sums = tree_sum(now[4:8])
    rz0, z0q = unpack(sums0[0:1, :], 0), unpack(sums0[0:1, :], 1)
    rz1, z1p, z1q, z0p = (unpack(sums[0:1], k) for k in range(4))
    rbr, rbq, rbp = (unpack(sums[1:2], k) for k in range(3))
    qbq, qbp, pbp = (unpack(sums[2:3], k) for k in range(3))
    alpha0 = rz0 / z0q
    beta0 = rz1 / rz0
    alpha1 = rz1 / (z1p + beta0 * (z1q + z0p) + beta0 * beta0 * z0q)
    image = p[...] + beta0 * q[...]
    r_out[...] = res[...] - alpha1 * image
    x_out[...] = alpha0 * z0[...] + alpha1 * (z1[...] + beta0 * z0[...])
    leaf_part = (
        rbr
        - 2.0 * alpha1 * (rbp + beta0 * rbq)
        + alpha1 * alpha1 * (pbp + 2.0 * beta0 * qbp + beta0 * beta0 * qbq)
    )
    low = lane((COLS, PTS)) < RANK
    now = [table1[t] - alpha1 * (now[t] + beta0 * table_q[t]) for t in range(NT)]
    top = jnp.where(low, tree_sum(now[0:4]), 0.0)
    squares = top * top + tree_sum([jnp.where(low, 0.0, v * v) for v in now])
    beta1 = (leaf_part + jnp.sum(squares, 1, keepdims=True)) / rz1
    for k, v in enumerate((alpha0, alpha1, beta0, beta1)):
        coefs[k // 2, k % 2 : k % 2 + 1, :] = pack([v])[:, 0:COLS]


def gather(block, axes):
    return lax.all_to_all(jnp.broadcast_to(block[None], (NG,) + block.shape), axes, 0, 0, tiled=True)


def scatter(parts):
    return lax.all_to_all(parts, GB, 0, 0, tiled=True)


def on_device(points, inverse_length, target, probe_bits, leaf_inverse, top_basis, sub_basis):
    vec = ((COLS, PTS), F32)
    square = ((PTS, PTS), F32)
    table = ((NT, COLS, PTS), F32)
    block = ((NG * PTS, NG * PTS), BF16)
    parts = ((NG, COLS, PTS), F32)
    wide = ((COLS + 8, PTS), F32)
    dma = pltpu.SemaphoreType.DMA
    where = lax.axis_index(("zl",) + GA).astype(jnp.int32).reshape(1)
    send, rhs, basis, leaf, leaf_part, marks = call(
        start_kernel,
        [((2 * COLS, PTS), F32), vec, square, square, vec, ((NG + 8, PTS), F32)],
        where, inverse_length, points, target[None, :], probe_bits, top_basis, sub_basis, leaf_inverse,
        spaces=[SMEM] + [HBM] * 7,
        scratch=[
            pltpu.VMEM((COLS, PTS), F32), pltpu.VMEM((1, PTS), F32), pltpu.VMEM((COLS - 1, PTS), jnp.int32),
            pltpu.SMEM((COLS,), F32), dma((7,)),
        ],
        name="start",
    )
    got_b = gather(send, GB)
    (send,) = call(fold0_kernel, [((SEND0, PTS), F32)], got_b, send, basis, leaf_part, name="fold0")
    got_a = gather(send, GA)
    high, low = call(
        matern_kernel, [block, block], got_a, got_b, limit=24 << 20,
        scratch=[pltpu.VMEM((NG * PTS, PTS), BF16), pltpu.VMEM((PTS, NG * PTS), BF16)],
        name="matern",
    )
    out, z0, table0 = call(
        first_kernel, [parts, vec, table], marks, got_a, high, low,
        limit=24 << 20, scratch=[pltpu.VMEM((NG, COLS, PTS), F32)], name="first",
    )
    q, leaf_part, send = call(image0_kernel, [vec, vec, wide], scatter(out), z0, rhs, basis, leaf, name="image0")
    (send,) = call(fold1_kernel, [((3 * COLS, PTS), F32)], gather(send, GB), leaf_part, name="fold1")
    out, z1, res, table1, table_q, sums0 = call(
        second_kernel, [parts, vec, vec, table, table, ((8, PTS), F32)],
        marks, gather(send, GA), got_a, table0, rhs, q, high, low,
        limit=24 << 20, scratch=[pltpu.VMEM((NG, COLS, PTS), F32)], name="second",
    )
    p, send = call(image1_kernel, [vec, wide], scatter(out), z1, z0, res, q, leaf, basis, name="image1")
    (send,) = call(fold2_kernel, [((2 * COLS, PTS), F32)], gather(send, GB), name="fold2")
    x_out, r_out, coefs = call(
        finish_kernel, [vec, vec, ((2, 2, COLS), F32)],
        gather(send, GA), z0, z1, res, q, p, table1, table_q, sums0, name="finish",
    )
    return x_out, r_out, coefs


def solution(mesh):
    named = Mesh(mesh.devices.reshape(2, 4, 4, 4, 2), AXES)
    return jax.shard_map(
        on_device,
        mesh=named,
        in_specs=(P(None, AXES), P(), P(AXES), P(None, AXES), P(AXES, None), P(None, AXES), P(None, AXES)),
        out_specs=(P(None, AXES), P(None, AXES), P()),
        check_vma=False,
    )
```

profile of v0, /device:TPU:1, one launch (start us, length us, event | category | flops | bytes accessed | tf_op | source)
XLA Modules:
  0.0 144.7 jit_solution(4509555706529719133)
XLA Ops:
  0.6 1.3 start.1
  2.0 21.6 %all_to_all.40.got.right = f32[16,32,128]{2,1,0:T(8,128)S(1)} all-to-all(f32[16,32,128]{2,1,0:T(8,128)S(1)} %broadcast_in_dim.15), channel_id=1, replica_groups=mesh['zl'=2,'y'=4,'zh'=4,'x'=4,'c'=2] {'zl','zh','c'}, dimensions={0} | all-to-all | bytes 524288 | tf_op jit(solution)/shard_map/all_to_all | solution.py:321
  23.6 0.1 broadcast_in_dim.16
  23.8 30.3 %all_to_all.41.left.got_a.got0 = f32[16,192,128]{2,1,0:T(8,128)S(1)} all-to-all(f32[16,192,128]{2,1,0:T(8,128)S(1)} %broadcast_in_dim.16), channel_id=1, replica_groups=mesh['zl'=2,'y'=4,'zh'=4,'x'=4,'c'=2] {'y','x'}, dimensions={0} | all-to-all | bytes 3145728 | tf_op jit(solution)/shard_map/all_to_all | solution.py:321
  54.1 8.4 %matern.1 = (bf16[2048,2048]{1,0:T(8,128)(2,1)S(1)}, bf16[2048,2048]{1,0:T(8,128)(2,1)S(1)}) custom-call(f32[16,192,128]{2,1,0:T(8,128)S(1)} %all_to_all.41.left.got_a.got0, f32[16,32,128]{2,1,0:T(8,128)S(1)} %all_to_all.40.got.right), custom_call_target="tpu_custom_call" | custom-call | tf_op jit(solution)/shard_map/matern/pallas_call | solution.py:89
  62.5 2.8 %first.1 = (f32[16,16,128]{2,1,0:T(8,128)S(1)}, f32[16,128]{1,0:T(8,128)S(1)}, f32[8,16,128]{2,1,0:T(8,128)S(1)}) custom-call(f32[24,128]{1,0:T(8,128)S(1)} %get-tuple-element.25.marks, f32[16,192,128]{2,1,0:T(8,128)S(1)} %all_to_all.41.left.got_a.got0, bf16[2048,2048]{1,0:T(8,128)(2,1)S(1)} %get-tuple-element.29.high, ...), custom_call_target="tpu_custom_call" | custom-call | tf_op jit(solution)/shard_map/first/pallas_call | solution.py:89
  65.3 11.9 %all_to_all.42.got = f32[16,16,128]{2,1,0:T(8,128)S(1)} all-to-all(f32[16,16,128]{2,1,0:T(8,128)S(1)} %get-tuple-element.31), channel_id=1, replica_groups=mesh['zl'=2,'y'=4,'zh'=4,'x'=4,'c'=2] {'zl','zh','c'}, dimensions={0} | all-to-all | bytes 262144 | tf_op jit(solution)/shard_map/all_to_all | solution.py:325
  77.2 0.3 image0.1
  77.6 13.0 %all_to_all.43.got = f32[16,24,128]{2,1,0:T(8,128)S(1)} all-to-all(f32[16,24,128]{2,1,0:T(8,128)S(1)} %broadcast_in_dim.17), channel_id=1, replica_groups=mesh['zl'=2,'y'=4,'zh'=4,'x'=4,'c'=2] {'zl','zh','c'}, dimensions={0} | all-to-all | bytes 393216 | tf_op jit(solution)/shard_map/all_to_all | solution.py:321
  90.6 13.1 %all_to_all.44.got = f32[16,48,128]{2,1,0:T(8,128)S(1)} all-to-all(f32[16,48,128]{2,1,0:T(8,128)S(1)} %broadcast_in_dim.18), channel_id=1, replica_groups=mesh['zl'=2,'y'=4,'zh'=4,'x'=4,'c'=2] {'y','x'}, dimensions={0} | all-to-all | bytes 786432 | tf_op jit(solution)/shard_map/all_to_all | solution.py:321
  103.7 2.9 %second.1 = (f32[16,16,128]{2,1,0:T(8,128)S(1)}, f32[16,128]{1,0:T(8,128)S(1)}, f32[16,128]{1,0:T(8,128)S(1)}, f32[8,16,128]{2,1,0:T(8,128)S(1)}, f32[8,16,128]{2,1,0:T(8,128)S(1)}, /*index=5*/f32[8,128]{1,0:T(8,128)S(1)}) custom-call(f32[24,128]{1,0:T(8,128)S(1)} %get-tuple-element.25.marks, f32[16,48,128]{2,1,0:T(8,128)S(1)} %all_to_all.44.got, ...), custom_call_target="tpu_custom_call" | custom-call | tf_op jit(solution)/shard_map/second/pallas_call | solution.py:89
  106.6 12.1 %all_to_all.45.got = f32[16,16,128]{2,1,0:T(8,128)S(1)} all-to-all(f32[16,16,128]{2,1,0:T(8,128)S(1)} %get-tuple-element.39), channel_id=1, replica_groups=mesh['zl'=2,'y'=4,'zh'=4,'x'=4,'c'=2] {'zl','zh','c'}, dimensions={0} | all-to-all | bytes 262144 | tf_op jit(solution)/shard_map/all_to_all | solution.py:325
  118.7 0.6 image1.1
  119.3 13.0 %all_to_all.46.got = f32[16,24,128]{2,1,0:T(8,128)S(1)} all-to-all(f32[16,24,128]{2,1,0:T(8,128)S(1)} %broadcast_in_dim.19), channel_id=1, replica_groups=mesh['zl'=2,'y'=4,'zh'=4,'x'=4,'c'=2] {'zl','zh','c'}, dimensions={0} | all-to-all | bytes 393216 | tf_op jit(solution)/shard_map/all_to_all | solution.py:321
  132.3 11.6 %all_to_all.47.got = f32[16,32,128]{2,1,0:T(8,128)S(1)} all-to-all(f32[16,32,128]{2,1,0:T(8,128)S(1)} %broadcast_in_dim.20), channel_id=1, replica_groups=mesh['zl'=2,'y'=4,'zh'=4,'x'=4,'c'=2] {'y','x'}, dimensions={0} | all-to-all | bytes 524288 | tf_op jit(solution)/shard_map/all_to_all | solution.py:321
  143.9 0.8 finish.1
  (8 shorter events, 0.2 us)
where the time goes:
time: 145 us
  blocking collectives  127 us (88%)
  Pallas kernels  17.1 us (12%)
    all_to_all x6, blocking collectives, gather(): lax.all_to_all(jnp.broadcast_to(block[None], (NG,) + block.shape), axes,...  103 us
    all_to_all x2, blocking collectives, scatter(): return lax.all_to_all(parts, GB, 0, 0, tiled=True)  24 us
    pallas_call x10, Pallas kernels, call(): pl.pallas_call(kernel, out_shape=[m(s, d) if m is HBM else jax.ShapeDtype...  17.1 us

commit v1 on v0

--- a/solution.py
+++ b/solution.py
@@ -97,9 +97,9 @@
     )(*args)
 
 
-SEND0 = 12 * COLS
-BASES = slice(3 * COLS, 3 * COLS + PTS)
-LEAF_PART = slice(11 * COLS, 12 * COLS)
+SEND0 = 5 * COLS // 2 + PTS + COLS
+BASES = slice(5 * COLS // 2, 5 * COLS // 2 + PTS)
+LEAF_PART = slice(SEND0 - COLS, SEND0)
 
 
 def start_kernel(where, inv_h, points_h, target_h, bits_h, top_h, sub_h, leaf_h, send, rhs, basis, leaf, leaf_part, marks, points, target, bits, inv, sems):
@@ -135,31 +135,50 @@
     leaf_part[...] = dot_nt(rhs[...], leaf[...])
 
 
-def fold_tiles(got, first, scalars, send, at):
+def pack_half(tile):
+    return jnp.where(lane((8, PTS)) < RANK, pltpu.roll(tile[0:8], RANK, 1), tile[8:16])
+
+
+def unpack_half(packed):
+    return jnp.concatenate([pltpu.roll(packed, RANK, 1), packed], 0)
+
+
+def fold0_kernel(got, own, basis, leaf_part, send):
     low = lane((COLS, PTS)) < RANK
-    zero = tree_sum([got[j, first : first + COLS] for j in range(NG // 2)])
-    one = tree_sum([got[j, first : first + COLS] for j in range(NG // 2, NG)])
-    send[at : at + COLS, :] = jnp.where(low, zero + one, zero)
-    send[at + COLS : at + 2 * COLS, :] = jnp.where(low, 0.0, one)
-    if scalars:
-        own = tree_sum([got[j, scalars : scalars + 8] for j in range(NG)])
-        send[at + COLS : at + COLS + 8, :] = jnp.where(low[0:8], own, one[0:8])
-
-
-def fold0_kernel(got, own, basis, leaf_part, send):
+    zero = tree_sum([got[j, COLS : 2 * COLS] for j in range(NG // 2)])
+    one = tree_sum([got[j, COLS : 2 * COLS] for j in range(NG // 2, NG)])
     send[0:COLS, :] = own[0:COLS, :]
-    fold_tiles(got, COLS, 0, send, COLS)
+    send[COLS : 2 * COLS, :] = jnp.where(low, zero + one, zero)
+    send[2 * COLS : 5 * COLS // 2, :] = pack_half(one)
     send[BASES, :] = basis[...]
     send[LEAF_PART, :] = leaf_part[...]
 
 
-def fold1_kernel(got, leaf_part, send):
-    fold_tiles(got, 0, COLS, send, 0)
+def fold_rows(got, rows, send, zero, one):
+    for r in range(COLS):
+        zero[r : r + 1, :] = tree_sum([got[j, r] for j in range(NG // 2)])
+        one[r : r + 1, :] = tree_sum([got[j, r] for j in range(NG // 2, NG)])
+    own = tile_rows([tree_sum([got[j, r] for j in range(NG)]) for r in range(COLS, rows)])
+    low = lane((COLS, PTS)) < RANK
+    send[0:COLS, :] = jnp.where(low, zero[...] + one[...], zero[...])
+    send[COLS : 2 * COLS, :] = jnp.where(low, 0.0, one[...])
+    send[COLS : COLS + 8, :] = jnp.where(low[0:8], own, one[0:8, :])
+
+
+def fold1_kernel(got, leaf_part, send, zero, one):
+    fold_rows(got, COLS + 1, send, zero, one)
     send[2 * COLS : 3 * COLS, :] = leaf_part[...]
 
 
-def fold2_kernel(got, send):
-    fold_tiles(got, 0, COLS, send, 0)
+def fold2_kernel(got, send, zero, one):
+    fold_rows(got, COLS + 3, send, zero, one)
+
+
+def send_rows(send, coefs, rows):
+    for r in range(COLS):
+        send[r] = coefs[r : r + 1, :]
+    for k, row in enumerate(rows):
+        send[COLS + k] = row
 
 
 def sum_tiles(got, first):
@@ -208,28 +227,47 @@
     return jnp.concatenate(parts + [tail, jnp.zeros((PTS - 6 * COLS - 8, PTS), F32)], 0)
 
 
-def matern_kernel(left, right, high, low, left_f, right_f):
+def first_kernel(marks, got_a, got_b, high, low, out, z, table, directions, left_f, right_f, both, acc):
+    tops = [tree_sum([got_a[4 * y + x, COLS : 2 * COLS] for x in range(4)]) for y in range(4)]
+    subs = [tree_sum([got_a[4 * y + x, 2 * COLS : 5 * COLS // 2] for x in range(4)]) for y in range(4)]
+    now = tops + [unpack_half(v) for v in subs]
+    for t in range(NT):
+        table[t] = now[t]
+    column_directions(marks, now, lambda j: got_a[j, LEAF_PART], got_a, directions)
+    z[...] = own_direction(marks, directions)
     for j in range(NG):
         at = slice(j * PTS, (j + 1) * PTS)
-        right_f[:, at] = features(right[j, 0:COLS] * COORD_SCALE, False).astype(BF16)
-        left_f[at, :] = features(left[j, 0:COLS] * COORD_SCALE, True).T.astype(BF16)
+        right_f[:, at] = features(got_b[j, 0:COLS] * COORD_SCALE, False).astype(BF16)
+        left_f[at, :] = features(got_a[j, 0:COLS] * COORD_SCALE, True).T.astype(BF16)
+        v = directions[j] * LEAD
+        v_high = v.astype(BF16)
+        both[j] = jnp.concatenate([v_high, (v - v_high.astype(F32)).astype(BF16)], 0)
+    acc[...] = jnp.zeros_like(acc)
     height, width = 1024, 256
+    blocks = height // PTS
 
     def step(i, carry):
         rows = pl.ds(pl.multiple_of(i * height, height), height)
-        lhs = left_f[rows, :]
+        points = left_f[rows, :]
+        vectors = jnp.concatenate([both[i * blocks + b] for b in range(blocks)], 1)
         for j in range(0, NG * PTS, width):
-            s = jnp.dot(lhs, right_f[:, j : j + width], preferred_element_type=F32)
+            s = jnp.dot(points, right_f[:, j : j + width], preferred_element_type=F32)
             s = jnp.maximum(s, 1e-30)
             v = s * lax.rsqrt(s)
             w = v + SHIFT
             k = (w * w + REST) * jnp.exp2(-v)
-            h = k.astype(BF16)
-            high[rows, j : j + width] = h
-            low[rows, j : j + width] = (k - h.astype(F32)).astype(BF16)
+            k_high = k.astype(BF16)
+            k_low = (k - k_high.astype(F32)).astype(BF16)
+            high[rows, j : j + width] = k_high
+            low[rows, j : j + width] = k_low
+            r = jnp.dot(vectors, k_high, preferred_element_type=F32)
+            r = r[0:COLS] + r[COLS:] + jnp.dot(vectors[0:COLS], k_low, preferred_element_type=F32)
+            acc[:, j : j + width] += r
         return carry
 
-    lax.fori_loop(0, NG * PTS // height, step, 0)
+    lax.fori_loop(0, NG // blocks, step, 0)
+    for b in range(NG):
+        out[b] = acc[:, b * PTS : (b + 1) * PTS]
 
 
 def matvec(directions, high, low, out):
@@ -244,23 +282,15 @@
             out[j // PTS + b] = r[:, b * PTS : (b + 1) * PTS]
 
 
-def first_kernel(marks, got_a, high, low, out, z, table, directions):
-    now = sum_tiles(got_a, COLS)
-    for t in range(NT):
-        table[t] = now[t]
-    column_directions(marks, now, lambda j: got_a[j, LEAF_PART], got_a, directions)
-    z[...] = own_direction(marks, directions)
-    matvec(directions, high, low, out)
-
-
 def image0_kernel(got, z, rhs, basis, leaf, q, leaf_part, send):
     q[...] = tree_sum([got[j] for j in range(NG)]) + NOISE * z[...]
-    send[0:COLS, :] = dot_nt(q[...], basis[...])
-    send[COLS:, :] = tile_rows([pack([rowdot(rhs[...], z[...]), rowdot(z[...], q[...])])])
+    send_rows(send, dot_nt(q[...], basis[...]), [pack([rowdot(rhs[...], z[...]), rowdot(z[...], q[...])])])
     leaf_part[...] = dot_nt(q[...], leaf[...])
 
 
-def second_kernel(marks, got, got0, table0, rhs, q, high, low, out, z, res, table, table_q, sums, directions):
+def second_kernel(
+    marks, got, got0, table0, rhs, q, leaf_rhs, leaf_q, high, low, out, z, res, leaf_res, table, table_q, sums, directions
+):
     now = sum_tiles(got, 0)
     total = tree_sum(now[4:8])
     sums[...] = total[0:8]
@@ -274,20 +304,20 @@
     )
     z[...] = own_direction(marks, directions)
     res[...] = rhs[...] - alpha * q[...]
+    leaf_res[...] = leaf_rhs[...] - alpha * leaf_q[...]
     matvec(directions, high, low, out)
 
 
-def image1_kernel(got, z1, z0, res, q, leaf, basis, p, send):
+def image1_kernel(got, z1, z0, res, q, leaf_res, leaf_q, leaf, basis, p, send):
     p[...] = tree_sum([got[j] for j in range(NG)]) + NOISE * z1[...]
-    send[0:COLS, :] = dot_nt(p[...], basis[...])
     rv, qv, pv, zv = res[...], q[...], p[...], z1[...]
-    rb, qb, pb = (dot_nt(v, leaf[...]) for v in (rv, qv, pv))
+    rb, qb, pb = leaf_res[...], leaf_q[...], dot_nt(pv, leaf[...])
     rows = [
         pack([rowdot(rv, zv), rowdot(zv, pv), rowdot(zv, qv), rowdot(z0[...], pv)]),
         pack([rowdot(rv, rb), rowdot(rv, qb), rowdot(rv, pb)]),
         pack([rowdot(qv, qb), rowdot(qv, pb), rowdot(pv, pb)]),
     ]
-    send[COLS:, :] = tile_rows(rows)
+    send_rows(send, dot_nt(pv, basis[...]), rows)
 
 
 def finish_kernel(got, z0, z1, res, q, p, table1, table_q, sums0, x_out, r_out, coefs):
@@ -331,7 +361,9 @@
     table = ((NT, COLS, PTS), F32)
     block = ((NG * PTS, NG * PTS), BF16)
     parts = ((NG, COLS, PTS), F32)
-    wide = ((COLS + 8, PTS), F32)
+    rows1 = ((COLS + 1, 1, PTS), F32)
+    rows2 = ((COLS + 3, 1, PTS), F32)
+    two = [pltpu.VMEM((COLS, PTS), F32)] * 2
     dma = pltpu.SemaphoreType.DMA
     where = lax.axis_index(("zl",) + GA).astype(jnp.int32).reshape(1)
     send, rhs, basis, leaf, leaf_part, marks = call(
@@ -348,24 +380,25 @@
     got_b = gather(send, GB)
     (send,) = call(fold0_kernel, [((SEND0, PTS), F32)], got_b, send, basis, leaf_part, name="fold0")
     got_a = gather(send, GA)
-    high, low = call(
-        matern_kernel, [block, block], got_a, got_b, limit=24 << 20,
-        scratch=[pltpu.VMEM((NG * PTS, PTS), BF16), pltpu.VMEM((PTS, NG * PTS), BF16)],
-        name="matern",
-    )
-    out, z0, table0 = call(
-        first_kernel, [parts, vec, table], marks, got_a, high, low,
-        limit=24 << 20, scratch=[pltpu.VMEM((NG, COLS, PTS), F32)], name="first",
-    )
-    q, leaf_part, send = call(image0_kernel, [vec, vec, wide], scatter(out), z0, rhs, basis, leaf, name="image0")
-    (send,) = call(fold1_kernel, [((3 * COLS, PTS), F32)], gather(send, GB), leaf_part, name="fold1")
-    out, z1, res, table1, table_q, sums0 = call(
-        second_kernel, [parts, vec, vec, table, table, ((8, PTS), F32)],
-        marks, gather(send, GA), got_a, table0, rhs, q, high, low,
+    high, low, out, z0, table0 = call(
+        first_kernel, [block, block, parts, vec, table], marks, got_a, got_b, limit=24 << 20,
+        scratch=[
+            pltpu.VMEM((NG, COLS, PTS), F32), pltpu.VMEM((NG * PTS, PTS), BF16), pltpu.VMEM((PTS, NG * PTS), BF16),
+            pltpu.VMEM((NG, 2 * COLS, PTS), BF16), pltpu.VMEM((COLS, NG * PTS), F32),
+        ],
+        name="first",
+    )
+    q, leaf_q, send = call(image0_kernel, [vec, vec, rows1], scatter(out), z0, rhs, basis, leaf, name="image0")
+    (send,) = call(fold1_kernel, [((3 * COLS, PTS), F32)], gather(send, GB), leaf_q, scratch=two, name="fold1")
+    out, z1, res, leaf_res, table1, table_q, sums0 = call(
+        second_kernel, [parts, vec, vec, vec, table, table, ((8, PTS), F32)],
+        marks, gather(send, GA), got_a, table0, rhs, q, leaf_part, leaf_q, high, low,
         limit=24 << 20, scratch=[pltpu.VMEM((NG, COLS, PTS), F32)], name="second",
     )
-    p, send = call(image1_kernel, [vec, wide], scatter(out), z1, z0, res, q, leaf, basis, name="image1")
-    (send,) = call(fold2_kernel, [((2 * COLS, PTS), F32)], gather(send, GB), name="fold2")
+    p, send = call(
+        image1_kernel, [vec, rows2], scatter(out), z1, z0, res, q, leaf_res, leaf_q, leaf, basis, name="image1"
+    )
+    (send,) = call(fold2_kernel, [((2 * COLS, PTS), F32)], gather(send, GB), scratch=two, name="fold2")
     x_out, r_out, coefs = call(
         finish_kernel, [vec, vec, ((2, 2, COLS), F32)],
         gather(send, GA), z0, z1, res, q, p, table1, table_q, sums0, name="finish",

time: 145 us -> 140 us (0.966)
  blocking collectives: 127 us -> 123 us
  Pallas kernels: 17.1 us -> 15.2 us
    all_to_all x6, blocking collectives: 103 us -> 98.7 us  [gather(): lax.all_to_all(jnp.broadcast_to(block[None], (NG,) + block.shape), axes,...]
    pallas_call x10 -> x9, Pallas kernels: 17.1 us -> 15.2 us  [call(): pl.pallas_call(kernel, out_shape=[m(s, d) if m is HBM else jax.ShapeDtype...]
where the time goes in v1:
time: 140 us
  blocking collectives  123 us (88%)
  Pallas kernels  15.2 us (11%)
    all_to_all x6, blocking collectives, gather(): lax.all_to_all(jnp.broadcast_to(block[None], (NG,) + block.shape), axes,...  98.7 us
    all_to_all x2, blocking collectives, scatter(): return lax.all_to_all(parts, GB, 0, 0, tiled=True)  24.6 us
    pallas_call x9, Pallas kernels, call(): pl.pallas_call(kernel, out_shape=[m(s, d) if m is HBM else jax.ShapeDtype...  15.2 us

profile of v1, /device:TPU:1, one launch (start us, length us, event | category | flops | bytes accessed | tf_op | source)
XLA Modules:
  0.0 139.6 jit_solution(5222806401220924245)
XLA Ops:
  0.6 1.3 start.1
  2.0 21.6 %all_to_all.40.got.got_b = f32[16,32,128]{2,1,0:T(8,128)S(1)} all-to-all(f32[16,32,128]{2,1,0:T(8,128)S(1)} %broadcast_in_dim.19), channel_id=1, replica_groups=mesh['zl'=2,'y'=4,'zh'=4,'x'=4,'c'=2] {'zl','zh','c'}, dimensions={0} | all-to-all | bytes 524288 | tf_op jit(solution)/shard_map/all_to_all | solution.py:351
  23.6 0.1 fold0.1
  23.7 0.1 broadcast_in_dim.20
  23.8 29.5 %all_to_all.41.got_a.got0 = f32[16,184,128]{2,1,0:T(8,128)S(1)} all-to-all(f32[16,184,128]{2,1,0:T(8,128)S(1)} %broadcast_in_dim.20), channel_id=1, replica_groups=mesh['zl'=2,'y'=4,'zh'=4,'x'=4,'c'=2] {'y','x'}, dimensions={0} | all-to-all | bytes 3014656 | tf_op jit(solution)/shard_map/all_to_all | solution.py:351
  53.3 9.4 %first.1 = (bf16[2048,2048]{1,0:T(8,128)(2,1)S(1)}, bf16[2048,2048]{1,0:T(8,128)(2,1)S(1)}, f32[16,16,128]{2,1,0:T(8,128)S(1)}, f32[16,128]{1,0:T(8,128)S(1)}, f32[8,16,128]{2,1,0:T(8,128)S(1)}) custom-call(f32[24,128]{1,0:T(8,128)S(1)} %get-tuple-element.26.marks, f32[16,184,128]{2,1,0:T(8,128)S(1)} %all_to_all.41.got_a.got0, ...), custom_call_target="tpu_custom_call" | custom-call | tf_op jit(solution)/shard_map/first/pallas_call | solution.py:89
  62.6 11.9 %all_to_all.42.got = f32[16,16,128]{2,1,0:T(8,128)S(1)} all-to-all(f32[16,16,128]{2,1,0:T(8,128)S(1)} %get-tuple-element.30), channel_id=1, replica_groups=mesh['zl'=2,'y'=4,'zh'=4,'x'=4,'c'=2] {'zl','zh','c'}, dimensions={0} | all-to-all | bytes 262144 | tf_op jit(solution)/shard_map/all_to_all | solution.py:355
  74.5 0.3 image0.1
  74.8 0.1 broadcast_in_dim.22
  74.9 11.8 %all_to_all.43.got = f32[16,17,1,128]{3,2,1,0:T(1,128)S(1)} all-to-all(f32[16,17,1,128]{3,2,1,0:T(1,128)S(1)} %broadcast_in_dim.22), channel_id=1, replica_groups=mesh['zl'=2,'y'=4,'zh'=4,'x'=4,'c'=2] {'zl','zh','c'}, dimensions={0} | all-to-all | bytes 278528 | tf_op jit(solution)/shard_map/all_to_all | solution.py:351
  86.7 0.1 fold1.1
  86.8 12.6 %all_to_all.44.got = f32[16,48,128]{2,1,0:T(8,128)S(1)} all-to-all(f32[16,48,128]{2,1,0:T(8,128)S(1)} %broadcast_in_dim.23), channel_id=1, replica_groups=mesh['zl'=2,'y'=4,'zh'=4,'x'=4,'c'=2] {'y','x'}, dimensions={0} | all-to-all | bytes 786432 | tf_op jit(solution)/shard_map/all_to_all | solution.py:351
  99.4 2.9 %second.1 = (f32[16,16,128]{2,1,0:T(8,128)S(1)}, f32[16,128]{1,0:T(8,128)S(1)}, f32[16,128]{1,0:T(8,128)S(1)}, f32[16,128]{1,0:T(8,128)S(1)}, f32[8,16,128]{2,1,...) custom-call(f32[24,128]{1,0:T(8,128)S(1)} %get-tuple-element.26.marks, ...), custom_call_target="tpu_custom_call" | custom-call | tf_op jit(solution)/shard_map/second/pallas_call | solution.py:89
  102.2 12.8 %all_to_all.45.got = f32[16,16,128]{2,1,0:T(8,128)S(1)} all-to-all(f32[16,16,128]{2,1,0:T(8,128)S(1)} %get-tuple-element.40), channel_id=1, replica_groups=mesh['zl'=2,'y'=4,'zh'=4,'x'=4,'c'=2] {'zl','zh','c'}, dimensions={0} | all-to-all | bytes 262144 | tf_op jit(solution)/shard_map/all_to_all | solution.py:355
  115.0 0.4 image1.1
  115.4 0.1 broadcast_in_dim.50
  115.5 12.1 %all_to_all.46.got = f32[16,19,1,128]{3,2,1,0:T(1,128)S(1)} all-to-all(f32[16,19,1,128]{3,2,1,0:T(1,128)S(1)} %broadcast_in_dim.50), channel_id=1, replica_groups=mesh['zl'=2,'y'=4,'zh'=4,'x'=4,'c'=2] {'zl','zh','c'}, dimensions={0} | all-to-all | bytes 311296 | tf_op jit(solution)/shard_map/all_to_all | solution.py:351
  127.6 0.1 fold2.1
  127.7 11.1 %all_to_all.47.got = f32[16,32,128]{2,1,0:T(8,128)S(1)} all-to-all(f32[16,32,128]{2,1,0:T(8,128)S(1)} %broadcast_in_dim.51), channel_id=1, replica_groups=mesh['zl'=2,'y'=4,'zh'=4,'x'=4,'c'=2] {'y','x'}, dimensions={0} | all-to-all | bytes 524288 | tf_op jit(solution)/shard_map/all_to_all | solution.py:351
  138.9 0.8 finish.1
  (5 shorter events, 0.1 us)

commit v2 on v1

--- a/solution.py
+++ b/solution.py
@@ -97,6 +97,8 @@
     )(*args)
 
 
+HALF = COLS // 2
+COEFS = COLS + HALF
 SEND0 = 5 * COLS // 2 + PTS + COLS
 BASES = slice(5 * COLS // 2, 5 * COLS // 2 + PTS)
 LEAF_PART = slice(SEND0 - COLS, SEND0)
@@ -123,15 +125,20 @@
     place = where[0]
     hit = (row == lax.rem(place, NG)) | ((row >= NG) & (place >= NG))
     marks[...] = jnp.where(hit, 1.0, 0.0)
-    for m in moves:
+    for m in moves[4:6]:
         m.wait()
     scale = jnp.zeros((COLS, PTS), F32)
     for k in range(COLS):
         scale = jnp.where(sublane((COLS, PTS)) == k, inv[k], scale)
+    send[0:COLS, :] = points[...] * scale
+    for m in moves[0:2]:
+        m.wait()
     rhs[0:1, :] = target[...]
     rhs[1:COLS, :] = 2.0 * bits[...].astype(F32) - 1.0
-    send[0:COLS, :] = points[...] * scale
+    for m in moves[2:4]:
+        m.wait()
     send[COLS : 2 * COLS, :] = dot_nt(rhs[...], basis[...])
+    moves[6].wait()
     leaf_part[...] = dot_nt(rhs[...], leaf[...])
 
 
@@ -154,37 +161,38 @@
     send[LEAF_PART, :] = leaf_part[...]
 
 
-def fold_rows(got, rows, send, zero, one):
+def fold_rows(got, scalars, send, zero, one):
     for r in range(COLS):
         zero[r : r + 1, :] = tree_sum([got[j, r] for j in range(NG // 2)])
         one[r : r + 1, :] = tree_sum([got[j, r] for j in range(NG // 2, NG)])
-    own = tile_rows([tree_sum([got[j, r] for j in range(NG)]) for r in range(COLS, rows)])
     low = lane((COLS, PTS)) < RANK
     send[0:COLS, :] = jnp.where(low, zero[...] + one[...], zero[...])
-    send[COLS : 2 * COLS, :] = jnp.where(low, 0.0, one[...])
-    send[COLS : COLS + 8, :] = jnp.where(low[0:8], own, one[0:8, :])
+    send[COLS:COEFS, :] = pack_half(one[...])
+    for k in range(scalars):
+        send[COEFS + k : COEFS + k + 1, :] = tree_sum([got[j, COLS + k] for j in range(NG)])
 
 
 def fold1_kernel(got, leaf_part, send, zero, one):
-    fold_rows(got, COLS + 1, send, zero, one)
-    send[2 * COLS : 3 * COLS, :] = leaf_part[...]
+    fold_rows(got, 1, send, zero, one)
+    send[COEFS + 1 :, :] = leaf_part[...]
 
 
 def fold2_kernel(got, send, zero, one):
-    fold_rows(got, COLS + 3, send, zero, one)
+    fold_rows(got, 2, send, zero, one)
 
 
 def send_rows(send, coefs, rows):
-    for r in range(COLS):
-        send[r] = coefs[r : r + 1, :]
+    send[0:COLS, :] = coefs
     for k, row in enumerate(rows):
-        send[COLS + k] = row
-
-
-def sum_tiles(got, first):
-    return [
-        tree_sum([got[4 * y + x, at : at + COLS] for x in range(4)]) for at in (first, first + COLS) for y in range(4)
-    ]
+        send[COLS + k : COLS + k + 1, :] = row
+
+
+def sum_rows(got, scalars, held):
+    for y in range(4):
+        for r in range(COEFS):
+            held[y, r : r + 1, :] = tree_sum([got[4 * y + x, r] for x in range(4)])
+    table = [held[y, 0:COLS] for y in range(4)] + [unpack_half(held[y, COLS:COEFS]) for y in range(4)]
+    return table, [tree_sum([got[j, COEFS + k] for j in range(NG)]) for k in range(scalars)]
 
 
 def column_directions(marks, table, leaf_parts, got0, directions):
@@ -227,7 +235,7 @@
     return jnp.concatenate(parts + [tail, jnp.zeros((PTS - 6 * COLS - 8, PTS), F32)], 0)
 
 
-def first_kernel(marks, got_a, got_b, high, low, out, z, table, directions, left_f, right_f, both, acc):
+def first_kernel(marks, got_a, got_b, high, low, out, z, table, directions, left_f, right_f, both):
     tops = [tree_sum([got_a[4 * y + x, COLS : 2 * COLS] for x in range(4)]) for y in range(4)]
     subs = [tree_sum([got_a[4 * y + x, 2 * COLS : 5 * COLS // 2] for x in range(4)]) for y in range(4)]
     now = tops + [unpack_half(v) for v in subs]
@@ -242,32 +250,23 @@
         v = directions[j] * LEAD
         v_high = v.astype(BF16)
         both[j] = jnp.concatenate([v_high, (v - v_high.astype(F32)).astype(BF16)], 0)
-    acc[...] = jnp.zeros_like(acc)
-    height, width = 1024, 256
-    blocks = height // PTS
-
-    def step(i, carry):
-        rows = pl.ds(pl.multiple_of(i * height, height), height)
-        points = left_f[rows, :]
-        vectors = jnp.concatenate([both[i * blocks + b] for b in range(blocks)], 1)
-        for j in range(0, NG * PTS, width):
-            s = jnp.dot(points, right_f[:, j : j + width], preferred_element_type=F32)
-            s = jnp.maximum(s, 1e-30)
-            v = s * lax.rsqrt(s)
-            w = v + SHIFT
-            k = (w * w + REST) * jnp.exp2(-v)
-            k_high = k.astype(BF16)
-            k_low = (k - k_high.astype(F32)).astype(BF16)
-            high[rows, j : j + width] = k_high
-            low[rows, j : j + width] = k_low
-            r = jnp.dot(vectors, k_high, preferred_element_type=F32)
-            r = r[0:COLS] + r[COLS:] + jnp.dot(vectors[0:COLS], k_low, preferred_element_type=F32)
-            acc[:, j : j + width] += r
-        return carry
-
-    lax.fori_loop(0, NG // blocks, step, 0)
-    for b in range(NG):
-        out[b] = acc[:, b * PTS : (b + 1) * PTS]
+    points = left_f[...]
+    vectors = jnp.concatenate([both[j] for j in range(NG)], 1)
+    width = 256
+    for j in range(0, NG * PTS, width):
+        s = jnp.dot(points, right_f[:, j : j + width], preferred_element_type=F32)
+        s = jnp.maximum(s, 1e-30)
+        v = s * lax.rsqrt(s)
+        w = v + SHIFT
+        k = (w * w + REST) * jnp.exp2(-v)
+        k_high = k.astype(BF16)
+        k_low = (k - k_high.astype(F32)).astype(BF16)
+        high[:, j : j + width] = k_high
+        low[:, j : j + width] = k_low
+        r = jnp.dot(vectors, k_high, preferred_element_type=F32)
+        r = r[0:COLS] + r[COLS:] + jnp.dot(vectors[0:COLS], k_low, preferred_element_type=F32)
+        for b in range(width // PTS):
+            out[j // PTS + b] = r[:, b * PTS : (b + 1) * PTS]
 
 
 def matvec(directions, high, low, out):
@@ -289,18 +288,21 @@
 
 
 def second_kernel(
-    marks, got, got0, table0, rhs, q, leaf_rhs, leaf_q, high, low, out, z, res, leaf_res, table, table_q, sums, directions
+    marks, got, got0, table0, rhs, q, leaf_rhs, leaf_q, high, low,
+    out, z, res, leaf_res, table, table_q, sums, directions, held, leaf_parts,
 ):
-    now = sum_tiles(got, 0)
-    total = tree_sum(now[4:8])
-    sums[...] = total[0:8]
-    alpha = unpack(total[0:1], 0) / unpack(total[0:1], 1)
+    now, (total,) = sum_rows(got, 1, held)
+    for j in range(NG):
+        for r in range(COLS):
+            leaf_parts[j, r : r + 1, :] = got[j, COEFS + 1 + r]
+    sums[...] = total
+    alpha = unpack(total, 0) / unpack(total, 1)
     for t in range(NT):
         table_q[t] = now[t]
         now[t] = table0[t] - alpha * now[t]
         table[t] = now[t]
     column_directions(
-        marks, now, lambda j: got0[j, LEAF_PART] - alpha * got[j, 2 * COLS : 3 * COLS], got0, directions
+        marks, now, lambda j: got0[j, LEAF_PART] - alpha * leaf_parts[j], got0, directions
     )
     z[...] = own_direction(marks, directions)
     res[...] = rhs[...] - alpha * q[...]
@@ -313,26 +315,31 @@
     rv, qv, pv, zv = res[...], q[...], p[...], z1[...]
     rb, qb, pb = leaf_res[...], leaf_q[...], dot_nt(pv, leaf[...])
     rows = [
-        pack([rowdot(rv, zv), rowdot(zv, pv), rowdot(zv, qv), rowdot(z0[...], pv)]),
-        pack([rowdot(rv, rb), rowdot(rv, qb), rowdot(rv, pb)]),
-        pack([rowdot(qv, qb), rowdot(qv, pb), rowdot(pv, pb)]),
+        pack(
+            [
+                rowdot(rv, zv), rowdot(zv, pv), rowdot(zv, qv), rowdot(z0[...], pv),
+                rowdot(rv, rb), rowdot(rv, qb), rowdot(rv, pb), rowdot(qv, qb),
+            ]
+        ),
+        pack([rowdot(qv, pb), rowdot(pv, pb)]),
     ]
     send_rows(send, dot_nt(pv, basis[...]), rows)
 
 
-def finish_kernel(got, z0, z1, res, q, p, table1, table_q, sums0, x_out, r_out, coefs):
-    now = sum_tiles(got, 0)
-    sums = tree_sum(now[4:8])
-    rz0, z0q = unpack(sums0[0:1, :], 0), unpack(sums0[0:1, :], 1)
-    rz1, z1p, z1q, z0p = (unpack(sums[0:1], k) for k in range(4))
-    rbr, rbq, rbp = (unpack(sums[1:2], k) for k in range(3))
-    qbq, qbp, pbp = (unpack(sums[2:3], k) for k in range(3))
+def finish_kernel(got, z0, z1, res, q, p, table1, table_q, sums0, x_h, r_h, coefs, x_out, r_out, sems, held):
+    now, (sums, more) = sum_rows(got, 2, held)
+    rz0, z0q = unpack(sums0[...], 0), unpack(sums0[...], 1)
+    rz1, z1p, z1q, z0p, rbr, rbq, rbp, qbq = (unpack(sums, k) for k in range(8))
+    qbp, pbp = unpack(more, 0), unpack(more, 1)
     alpha0 = rz0 / z0q
     beta0 = rz1 / rz0
     alpha1 = rz1 / (z1p + beta0 * (z1q + z0p) + beta0 * beta0 * z0q)
     image = p[...] + beta0 * q[...]
     r_out[...] = res[...] - alpha1 * image
     x_out[...] = alpha0 * z0[...] + alpha1 * (z1[...] + beta0 * z0[...])
+    moves = (pltpu.make_async_copy(r_out, r_h, sems.at[0]), pltpu.make_async_copy(x_out, x_h, sems.at[1]))
+    for m in moves:
+        m.start()
     leaf_part = (
         rbr
         - 2.0 * alpha1 * (rbp + beta0 * rbq)
@@ -345,6 +352,8 @@
     beta1 = (leaf_part + jnp.sum(squares, 1, keepdims=True)) / rz1
     for k, v in enumerate((alpha0, alpha1, beta0, beta1)):
         coefs[k // 2, k % 2 : k % 2 + 1, :] = pack([v])[:, 0:COLS]
+    for m in moves:
+        m.wait()
 
 
 def gather(block, axes):
@@ -361,8 +370,9 @@
     table = ((NT, COLS, PTS), F32)
     block = ((NG * PTS, NG * PTS), BF16)
     parts = ((NG, COLS, PTS), F32)
-    rows1 = ((COLS + 1, 1, PTS), F32)
-    rows2 = ((COLS + 3, 1, PTS), F32)
+    rows1 = ((COLS + 1, PTS), F32)
+    rows2 = ((COLS + 2, PTS), F32)
+    held = pltpu.VMEM((4, COEFS, PTS), F32)
     two = [pltpu.VMEM((COLS, PTS), F32)] * 2
     dma = pltpu.SemaphoreType.DMA
     where = lax.axis_index(("zl",) + GA).astype(jnp.int32).reshape(1)
@@ -384,24 +394,26 @@
         first_kernel, [block, block, parts, vec, table], marks, got_a, got_b, limit=24 << 20,
         scratch=[
             pltpu.VMEM((NG, COLS, PTS), F32), pltpu.VMEM((NG * PTS, PTS), BF16), pltpu.VMEM((PTS, NG * PTS), BF16),
-            pltpu.VMEM((NG, 2 * COLS, PTS), BF16), pltpu.VMEM((COLS, NG * PTS), F32),
+            pltpu.VMEM((NG, 2 * COLS, PTS), BF16),
         ],
         name="first",
     )
     q, leaf_q, send = call(image0_kernel, [vec, vec, rows1], scatter(out), z0, rhs, basis, leaf, name="image0")
-    (send,) = call(fold1_kernel, [((3 * COLS, PTS), F32)], gather(send, GB), leaf_q, scratch=two, name="fold1")
+    (send,) = call(fold1_kernel, [((COEFS + 1 + COLS, PTS), F32)], gather(send[:, None], GB), leaf_q, scratch=two, name="fold1")
     out, z1, res, leaf_res, table1, table_q, sums0 = call(
-        second_kernel, [parts, vec, vec, vec, table, table, ((8, PTS), F32)],
-        marks, gather(send, GA), got_a, table0, rhs, q, leaf_part, leaf_q, high, low,
-        limit=24 << 20, scratch=[pltpu.VMEM((NG, COLS, PTS), F32)], name="second",
+        second_kernel, [parts, vec, vec, vec, table, table, ((1, PTS), F32)],
+        marks, gather(send[:, None], GA), got_a, table0, rhs, q, leaf_part, leaf_q, high, low,
+        limit=24 << 20,
+        scratch=[pltpu.VMEM((NG, COLS, PTS), F32), held, pltpu.VMEM((NG, COLS, PTS), F32)], name="second",
     )
     p, send = call(
         image1_kernel, [vec, rows2], scatter(out), z1, z0, res, q, leaf_res, leaf_q, leaf, basis, name="image1"
     )
-    (send,) = call(fold2_kernel, [((2 * COLS, PTS), F32)], gather(send, GB), scratch=two, name="fold2")
+    (send,) = call(fold2_kernel, [((COEFS + 2, PTS), F32)], gather(send[:, None], GB), scratch=two, name="fold2")
     x_out, r_out, coefs = call(
         finish_kernel, [vec, vec, ((2, 2, COLS), F32)],
-        gather(send, GA), z0, z1, res, q, p, table1, table_q, sums0, name="finish",
+        gather(send[:, None], GA), z0, z1, res, q, p, table1, table_q, sums0,
+        out_spaces=[HBM, HBM, VMEM], scratch=two + [dma((2,)), held], name="finish",
     )
     return x_out, r_out, coefs
 

time: 140 us -> 140 us (level)
  no operation moved by 1% of the time
where the time goes in v2:
time: 140 us
  blocking collectives  122 us (87%)
  Pallas kernels  16 us (11%)
    all_to_all x6, blocking collectives, gather(): lax.all_to_all(jnp.broadcast_to(block[None], (NG,) + block.shape), axes,...  97.4 us
    all_to_all x2, blocking collectives, scatter(): return lax.all_to_all(parts, GB, 0, 0, tiled=True)  24.7 us
    pallas_call x9, Pallas kernels, call(): pl.pallas_call(kernel, out_shape=[m(s, d) if m is HBM else jax.ShapeDtype...  16 us

profile of v2, /device:TPU:1, one launch (start us, length us, event | category | flops | bytes accessed | tf_op | source)
XLA Modules:
  0.0 139.5 jit_solution(8691162330502494300)
XLA Ops:
  0.6 1.5 %start.1 = (f32[32,128]{1,0:T(8,128)S(1)}, f32[16,128]{1,0:T(8,128)S(1)}, f32[128,128]{1,0:T(8,128)S(1)}, f32[128,128]{1,0:T(8,128)S(1)}, f32[16,128]{1,0:T(8,128)S(1)}, /*index=5*/f32[24,128]{1,0:T(8,128)S(1)}) custom-call(s32[1]{0:T(128)} %bitcast.where, f32[16]{0:T(128)} %inv_h.1, f32[16,128]{1,0:T(8,128)} %points_h.1, f32[1,128]{1,0:T(1,128)} %bitcast.2, ...), custom_call_target="tpu_custom_call" | custom-call | tf_op jit(solution)/shard_map/start/pallas_call | solution.py:89
  2.2 21.6 %all_to_all.40.got.got_b = f32[16,32,128]{2,1,0:T(8,128)S(1)} all-to-all(f32[16,32,128]{2,1,0:T(8,128)S(1)} %broadcast_in_dim.15), channel_id=1, replica_groups=mesh['zl'=2,'y'=4,'zh'=4,'x'=4,'c'=2] {'zl','zh','c'}, dimensions={0} | all-to-all | bytes 524288 | tf_op jit(solution)/shard_map/all_to_all | solution.py:360
  23.8 0.1 fold0.1
  23.9 0.1 broadcast_in_dim.16
  24.0 29.5 %all_to_all.41.got_a.got0 = f32[16,184,128]{2,1,0:T(8,128)S(1)} all-to-all(f32[16,184,128]{2,1,0:T(8,128)S(1)} %broadcast_in_dim.16), channel_id=1, replica_groups=mesh['zl'=2,'y'=4,'zh'=4,'x'=4,'c'=2] {'y','x'}, dimensions={0} | all-to-all | bytes 3014656 | tf_op jit(solution)/shard_map/all_to_all | solution.py:360
  53.5 9.2 %first.1 = (bf16[2048,2048]{1,0:T(8,128)(2,1)S(1)}, bf16[2048,2048]{1,0:T(8,128)(2,1)S(1)}, f32[16,16,128]{2,1,0:T(8,128)S(1)}, f32[16,128]{1,0:T(8,128)S(1)}, f32[8,16,128]{2,1,0:T(8,128)S(1)}) custom-call(f32[24,128]{1,0:T(8,128)S(1)} %get-tuple-element.26.marks, f32[16,184,128]{2,1,0:T(8,128)S(1)} %all_to_all.41.got_a.got0, ...), custom_call_target="tpu_custom_call" | custom-call | tf_op jit(solution)/shard_map/first/pallas_call | solution.py:89
  62.7 11.9 %all_to_all.42.got = f32[16,16,128]{2,1,0:T(8,128)S(1)} all-to-all(f32[16,16,128]{2,1,0:T(8,128)S(1)} %get-tuple-element.30), channel_id=1, replica_groups=mesh['zl'=2,'y'=4,'zh'=4,'x'=4,'c'=2] {'zl','zh','c'}, dimensions={0} | all-to-all | bytes 262144 | tf_op jit(solution)/shard_map/all_to_all | solution.py:364
  74.6 0.3 image0.1
  74.9 0.1 broadcast_in_dim.17
  75.0 11.8 %all_to_all.43.got = f32[16,17,1,128]{3,2,1,0:T(1,128)S(1)} all-to-all(f32[16,17,1,128]{3,2,1,0:T(1,128)S(1)} %broadcast_in_dim.17), channel_id=1, replica_groups=mesh['zl'=2,'y'=4,'zh'=4,'x'=4,'c'=2] {'zl','zh','c'}, dimensions={0} | all-to-all | bytes 278528 | tf_op jit(solution)/shard_map/all_to_all | solution.py:360
  86.8 0.1 fold1.1
  86.9 0.2 broadcast_in_dim.18
  87.1 11.9 %all_to_all.44.got = f32[16,41,1,128]{3,2,1,0:T(1,128)S(1)} all-to-all(f32[16,41,1,128]{3,2,1,0:T(1,128)S(1)} %broadcast_in_dim.18), channel_id=1, replica_groups=mesh['zl'=2,'y'=4,'zh'=4,'x'=4,'c'=2] {'y','x'}, dimensions={0} | all-to-all | bytes 671744 | tf_op jit(solution)/shard_map/all_to_all | solution.py:360
  99.0 2.9 %second.1 = (f32[16,16,128]{2,1,0:T(8,128)S(1)}, f32[16,128]{1,0:T(8,128)S(1)}, f32[16,128]{1,0:T(8,128)S(1)}, f32[16,128]{1,0:T(8,128)S(1)}, f32[8,16,128]{2,1,...) custom-call(f32[24,128]{1,0:T(8,128)S(1)} %get-tuple-element.26.marks, ...), custom_call_target="tpu_custom_call" | custom-call | tf_op jit(solution)/shard_map/second/pallas_call | solution.py:89
  101.9 12.8 %all_to_all.45.got = f32[16,16,128]{2,1,0:T(8,128)S(1)} all-to-all(f32[16,16,128]{2,1,0:T(8,128)S(1)} %get-tuple-element.40), channel_id=1, replica_groups=mesh['zl'=2,'y'=4,'zh'=4,'x'=4,'c'=2] {'zl','zh','c'}, dimensions={0} | all-to-all | bytes 262144 | tf_op jit(solution)/shard_map/all_to_all | solution.py:364
  114.6 0.4 image1.1
  115.0 0.1 broadcast_in_dim.19
  115.1 12.0 %all_to_all.46.got = f32[16,18,1,128]{3,2,1,0:T(1,128)S(1)} all-to-all(f32[16,18,1,128]{3,2,1,0:T(1,128)S(1)} %broadcast_in_dim.19), channel_id=1, replica_groups=mesh['zl'=2,'y'=4,'zh'=4,'x'=4,'c'=2] {'zl','zh','c'}, dimensions={0} | all-to-all | bytes 294912 | tf_op jit(solution)/shard_map/all_to_all | solution.py:360
  127.1 0.1 fold2.1
  127.2 0.1 broadcast_in_dim.20
  127.3 10.7 %all_to_all.47.got = f32[16,26,1,128]{3,2,1,0:T(1,128)S(1)} all-to-all(f32[16,26,1,128]{3,2,1,0:T(1,128)S(1)} %broadcast_in_dim.20), channel_id=1, replica_groups=mesh['zl'=2,'y'=4,'zh'=4,'x'=4,'c'=2] {'y','x'}, dimensions={0} | all-to-all | bytes 425984 | tf_op jit(solution)/shard_map/all_to_all | solution.py:360
  138.0 1.3 finish.1
  (1 shorter events, 0.0 us)

commit v3 on v2

--- a/solution.py
+++ b/solution.py
@@ -125,20 +125,15 @@
     place = where[0]
     hit = (row == lax.rem(place, NG)) | ((row >= NG) & (place >= NG))
     marks[...] = jnp.where(hit, 1.0, 0.0)
-    for m in moves[4:6]:
+    for m in moves:
         m.wait()
     scale = jnp.zeros((COLS, PTS), F32)
     for k in range(COLS):
         scale = jnp.where(sublane((COLS, PTS)) == k, inv[k], scale)
-    send[0:COLS, :] = points[...] * scale
-    for m in moves[0:2]:
-        m.wait()
     rhs[0:1, :] = target[...]
     rhs[1:COLS, :] = 2.0 * bits[...].astype(F32) - 1.0
-    for m in moves[2:4]:
-        m.wait()
+    send[0:COLS, :] = points[...] * scale
     send[COLS : 2 * COLS, :] = dot_nt(rhs[...], basis[...])
-    moves[6].wait()
     leaf_part[...] = dot_nt(rhs[...], leaf[...])
 
 
@@ -326,7 +321,7 @@
     send_rows(send, dot_nt(pv, basis[...]), rows)
 
 
-def finish_kernel(got, z0, z1, res, q, p, table1, table_q, sums0, x_h, r_h, coefs, x_out, r_out, sems, held):
+def finish_kernel(got, z0, z1, res, q, p, table1, table_q, sums0, x_out, r_out, coefs, held):
     now, (sums, more) = sum_rows(got, 2, held)
     rz0, z0q = unpack(sums0[...], 0), unpack(sums0[...], 1)
     rz1, z1p, z1q, z0p, rbr, rbq, rbp, qbq = (unpack(sums, k) for k in range(8))
@@ -337,9 +332,6 @@
     image = p[...] + beta0 * q[...]
     r_out[...] = res[...] - alpha1 * image
     x_out[...] = alpha0 * z0[...] + alpha1 * (z1[...] + beta0 * z0[...])
-    moves = (pltpu.make_async_copy(r_out, r_h, sems.at[0]), pltpu.make_async_copy(x_out, x_h, sems.at[1]))
-    for m in moves:
-        m.start()
     leaf_part = (
         rbr
         - 2.0 * alpha1 * (rbp + beta0 * rbq)
@@ -352,8 +344,6 @@
     beta1 = (leaf_part + jnp.sum(squares, 1, keepdims=True)) / rz1
     for k, v in enumerate((alpha0, alpha1, beta0, beta1)):
         coefs[k // 2, k % 2 : k % 2 + 1, :] = pack([v])[:, 0:COLS]
-    for m in moves:
-        m.wait()
 
 
 def gather(block, axes):
@@ -413,7 +403,7 @@
     x_out, r_out, coefs = call(
         finish_kernel, [vec, vec, ((2, 2, COLS), F32)],
         gather(send[:, None], GA), z0, z1, res, q, p, table1, table_q, sums0,
-        out_spaces=[HBM, HBM, VMEM], scratch=two + [dma((2,)), held], name="finish",
+        scratch=[held], name="finish",
     )
     return x_out, r_out, coefs
 

time: 140 us -> 139 us (level)
  no operation moved by 1% of the time
where the time goes in v3:
time: 139 us
  blocking collectives  122 us (88%)
  Pallas kernels  15.2 us (11%)
    all_to_all x6, blocking collectives, gather(): lax.all_to_all(jnp.broadcast_to(block[None], (NG,) + block.shape), axes,...  97.4 us
    all_to_all x2, blocking collectives, scatter(): return lax.all_to_all(parts, GB, 0, 0, tiled=True)  24.7 us
    pallas_call x9, Pallas kernels, call(): pl.pallas_call(kernel, out_shape=[m(s, d) if m is HBM else jax.ShapeDtype...  15.2 us

profile of v3, /device:TPU:1, one launch (start us, length us, event | category | flops | bytes accessed | tf_op | source)
XLA Modules:
  0.0 138.6 jit_solution(10791061968719269366)
XLA Ops:
  0.6 1.3 start.1
  2.0 21.6 %all_to_all.40.got.got_b = f32[16,32,128]{2,1,0:T(8,128)S(1)} all-to-all(f32[16,32,128]{2,1,0:T(8,128)S(1)} %broadcast_in_dim.15), channel_id=1, replica_groups=mesh['zl'=2,'y'=4,'zh'=4,'x'=4,'c'=2] {'zl','zh','c'}, dimensions={0} | all-to-all | bytes 524288 | tf_op jit(solution)/shard_map/all_to_all | solution.py:350
  23.6 0.1 fold0.1
  23.7 0.1 broadcast_in_dim.16
  23.8 29.5 %all_to_all.41.got_a.got0 = f32[16,184,128]{2,1,0:T(8,128)S(1)} all-to-all(f32[16,184,128]{2,1,0:T(8,128)S(1)} %broadcast_in_dim.16), channel_id=1, replica_groups=mesh['zl'=2,'y'=4,'zh'=4,'x'=4,'c'=2] {'y','x'}, dimensions={0} | all-to-all | bytes 3014656 | tf_op jit(solution)/shard_map/all_to_all | solution.py:350
  53.3 9.2 %first.1 = (bf16[2048,2048]{1,0:T(8,128)(2,1)S(1)}, bf16[2048,2048]{1,0:T(8,128)(2,1)S(1)}, f32[16,16,128]{2,1,0:T(8,128)S(1)}, f32[16,128]{1,0:T(8,128)S(1)}, f32[8,16,128]{2,1,0:T(8,128)S(1)}) custom-call(f32[24,128]{1,0:T(8,128)S(1)} %get-tuple-element.26.marks, f32[16,184,128]{2,1,0:T(8,128)S(1)} %all_to_all.41.got_a.got0, ...), custom_call_target="tpu_custom_call" | custom-call | tf_op jit(solution)/shard_map/first/pallas_call | solution.py:89
  62.5 11.9 %all_to_all.42.got = f32[16,16,128]{2,1,0:T(8,128)S(1)} all-to-all(f32[16,16,128]{2,1,0:T(8,128)S(1)} %get-tuple-element.30), channel_id=1, replica_groups=mesh['zl'=2,'y'=4,'zh'=4,'x'=4,'c'=2] {'zl','zh','c'}, dimensions={0} | all-to-all | bytes 262144 | tf_op jit(solution)/shard_map/all_to_all | solution.py:354
  74.4 0.3 image0.1
  74.7 0.1 broadcast_in_dim.17
  74.8 11.8 %all_to_all.43.got = f32[16,17,1,128]{3,2,1,0:T(1,128)S(1)} all-to-all(f32[16,17,1,128]{3,2,1,0:T(1,128)S(1)} %broadcast_in_dim.17), channel_id=1, replica_groups=mesh['zl'=2,'y'=4,'zh'=4,'x'=4,'c'=2] {'zl','zh','c'}, dimensions={0} | all-to-all | bytes 278528 | tf_op jit(solution)/shard_map/all_to_all | solution.py:350
  86.6 0.1 fold1.1
  86.7 0.2 broadcast_in_dim.18
  86.9 11.9 %all_to_all.44.got = f32[16,41,1,128]{3,2,1,0:T(1,128)S(1)} all-to-all(f32[16,41,1,128]{3,2,1,0:T(1,128)S(1)} %broadcast_in_dim.18), channel_id=1, replica_groups=mesh['zl'=2,'y'=4,'zh'=4,'x'=4,'c'=2] {'y','x'}, dimensions={0} | all-to-all | bytes 671744 | tf_op jit(solution)/shard_map/all_to_all | solution.py:350
  98.8 2.9 %second.1 = (f32[16,16,128]{2,1,0:T(8,128)S(1)}, f32[16,128]{1,0:T(8,128)S(1)}, f32[16,128]{1,0:T(8,128)S(1)}, f32[16,128]{1,0:T(8,128)S(1)}, f32[8,16,128]{2,1,...) custom-call(f32[24,128]{1,0:T(8,128)S(1)} %get-tuple-element.26.marks, ...), custom_call_target="tpu_custom_call" | custom-call | tf_op jit(solution)/shard_map/second/pallas_call | solution.py:89
  101.7 12.8 %all_to_all.45.got = f32[16,16,128]{2,1,0:T(8,128)S(1)} all-to-all(f32[16,16,128]{2,1,0:T(8,128)S(1)} %get-tuple-element.40), channel_id=1, replica_groups=mesh['zl'=2,'y'=4,'zh'=4,'x'=4,'c'=2] {'zl','zh','c'}, dimensions={0} | all-to-all | bytes 262144 | tf_op jit(solution)/shard_map/all_to_all | solution.py:354
  114.4 0.4 image1.1
  114.8 0.1 broadcast_in_dim.19
  114.9 12.0 %all_to_all.46.got = f32[16,18,1,128]{3,2,1,0:T(1,128)S(1)} all-to-all(f32[16,18,1,128]{3,2,1,0:T(1,128)S(1)} %broadcast_in_dim.19), channel_id=1, replica_groups=mesh['zl'=2,'y'=4,'zh'=4,'x'=4,'c'=2] {'zl','zh','c'}, dimensions={0} | all-to-all | bytes 294912 | tf_op jit(solution)/shard_map/all_to_all | solution.py:350
  126.9 0.1 fold2.1
  127.0 0.1 broadcast_in_dim.20
  127.1 10.7 %all_to_all.47.got = f32[16,26,1,128]{3,2,1,0:T(1,128)S(1)} all-to-all(f32[16,26,1,128]{3,2,1,0:T(1,128)S(1)} %broadcast_in_dim.20), channel_id=1, replica_groups=mesh['zl'=2,'y'=4,'zh'=4,'x'=4,'c'=2] {'y','x'}, dimensions={0} | all-to-all | bytes 425984 | tf_op jit(solution)/shard_map/all_to_all | solution.py:350
  137.8 0.8 finish.1
  (1 shorter events, 0.0 us)

commit v4 on v3

--- a/solution.py
+++ b/solution.py
@@ -173,7 +173,7 @@
 
 
 def fold2_kernel(got, send, zero, one):
-    fold_rows(got, 2, send, zero, one)
+    fold_rows(got, 1, send, zero, one)
 
 
 def send_rows(send, coefs, rows):
@@ -190,7 +190,7 @@
     return table, [tree_sum([got[j, COEFS + k] for j in range(NG)]) for k in range(scalars)]
 
 
-def column_directions(marks, table, leaf_parts, got0, directions):
+def column_directions(marks, table, leaf_parts, bases_high, bases_low, directions):
     low = lane((COLS, PTS)) < RANK
     odd = marks[NG : NG + 1, :] > 0.5
     top = tree_sum(table[0:4])
@@ -199,10 +199,8 @@
         high = coefs.astype(BF16)
         both = jnp.concatenate([high, (coefs - high.astype(F32)).astype(BF16)], 0)
         for j in range(4 * y, 4 * y + 4):
-            bases = got0[j, BASES]
-            first = bases.astype(BF16)
-            r = jnp.dot(both, first, preferred_element_type=F32)
-            r = r[0:COLS] + r[COLS:] + jnp.dot(high, (bases - first.astype(F32)).astype(BF16), preferred_element_type=F32)
+            r = jnp.dot(both, bases_high[j], preferred_element_type=F32)
+            r = r[0:COLS] + r[COLS:] + jnp.dot(high, bases_low[j], preferred_element_type=F32)
             directions[j] = leaf_parts(j) + r
 
 
@@ -230,13 +228,17 @@
     return jnp.concatenate(parts + [tail, jnp.zeros((PTS - 6 * COLS - 8, PTS), F32)], 0)
 
 
-def first_kernel(marks, got_a, got_b, high, low, out, z, table, directions, left_f, right_f, both):
+def first_kernel(marks, got_a, got_b, high, low, out, z, table, bases_high, bases_low, directions, left_f, right_f, both):
     tops = [tree_sum([got_a[4 * y + x, COLS : 2 * COLS] for x in range(4)]) for y in range(4)]
     subs = [tree_sum([got_a[4 * y + x, 2 * COLS : 5 * COLS // 2] for x in range(4)]) for y in range(4)]
     now = tops + [unpack_half(v) for v in subs]
     for t in range(NT):
         table[t] = now[t]
-    column_directions(marks, now, lambda j: got_a[j, LEAF_PART], got_a, directions)
+    for j in range(NG):
+        bases = got_a[j, BASES]
+        bases_high[j] = bases.astype(BF16)
+        bases_low[j] = (bases - bases.astype(BF16).astype(F32)).astype(BF16)
+    column_directions(marks, now, lambda j: got_a[j, LEAF_PART], bases_high, bases_low, directions)
     z[...] = own_direction(marks, directions)
     for j in range(NG):
         at = slice(j * PTS, (j + 1) * PTS)
@@ -278,12 +280,14 @@
 
 def image0_kernel(got, z, rhs, basis, leaf, q, leaf_part, send):
     q[...] = tree_sum([got[j] for j in range(NG)]) + NOISE * z[...]
-    send_rows(send, dot_nt(q[...], basis[...]), [pack([rowdot(rhs[...], z[...]), rowdot(z[...], q[...])])])
     leaf_part[...] = dot_nt(q[...], leaf[...])
+    send_rows(send, dot_nt(q[...], basis[...]), [
+        pack([rowdot(rhs[...], z[...]), rowdot(z[...], q[...]), rowdot(q[...], leaf_part[...])])
+    ])
 
 
 def second_kernel(
-    marks, got, got0, table0, rhs, q, leaf_rhs, leaf_q, high, low,
+    marks, got, got0, bases_high, bases_low, table0, rhs, q, leaf_rhs, leaf_q, high, low,
     out, z, res, leaf_res, table, table_q, sums, directions, held, leaf_parts,
 ):
     now, (total,) = sum_rows(got, 1, held)
@@ -297,7 +301,7 @@
         now[t] = table0[t] - alpha * now[t]
         table[t] = now[t]
     column_directions(
-        marks, now, lambda j: got0[j, LEAF_PART] - alpha * leaf_parts[j], got0, directions
+        marks, now, lambda j: got0[j, LEAF_PART] - alpha * leaf_parts[j], bases_high, bases_low, directions
     )
     z[...] = own_direction(marks, directions)
     res[...] = rhs[...] - alpha * q[...]
@@ -305,30 +309,22 @@
     matvec(directions, high, low, out)
 
 
-def image1_kernel(got, z1, z0, res, q, leaf_res, leaf_q, leaf, basis, p, send):
+def image1_kernel(got, z1, res, q, leaf_res, leaf_q, leaf, basis, p, send):
     p[...] = tree_sum([got[j] for j in range(NG)]) + NOISE * z1[...]
     rv, qv, pv, zv = res[...], q[...], p[...], z1[...]
     rb, qb, pb = leaf_res[...], leaf_q[...], dot_nt(pv, leaf[...])
-    rows = [
-        pack(
-            [
-                rowdot(rv, zv), rowdot(zv, pv), rowdot(zv, qv), rowdot(z0[...], pv),
-                rowdot(rv, rb), rowdot(rv, qb), rowdot(rv, pb), rowdot(qv, qb),
-            ]
-        ),
-        pack([rowdot(qv, pb), rowdot(pv, pb)]),
-    ]
+    pairs = ((rv, zv), (zv, pv), (zv, qv), (rv, rb), (rv, qb), (rv, pb), (qv, pb), (pv, pb))
+    rows = [pack([rowdot(a, b) for a, b in pairs])]
     send_rows(send, dot_nt(pv, basis[...]), rows)
 
 
 def finish_kernel(got, z0, z1, res, q, p, table1, table_q, sums0, x_out, r_out, coefs, held):
-    now, (sums, more) = sum_rows(got, 2, held)
-    rz0, z0q = unpack(sums0[...], 0), unpack(sums0[...], 1)
-    rz1, z1p, z1q, z0p, rbr, rbq, rbp, qbq = (unpack(sums, k) for k in range(8))
-    qbp, pbp = unpack(more, 0), unpack(more, 1)
+    now, (sums,) = sum_rows(got, 1, held)
+    rz0, z0q, qbq = (unpack(sums0[...], k) for k in range(3))
+    rz1, z1p, z1q, rbr, rbq, rbp, qbp, pbp = (unpack(sums, k) for k in range(8))
     alpha0 = rz0 / z0q
     beta0 = rz1 / rz0
-    alpha1 = rz1 / (z1p + beta0 * (z1q + z0p) + beta0 * beta0 * z0q)
+    alpha1 = rz1 / (z1p + 2.0 * beta0 * z1q + beta0 * beta0 * z0q)
     image = p[...] + beta0 * q[...]
     r_out[...] = res[...] - alpha1 * image
     x_out[...] = alpha0 * z0[...] + alpha1 * (z1[...] + beta0 * z0[...])
@@ -360,8 +356,8 @@
     table = ((NT, COLS, PTS), F32)
     block = ((NG * PTS, NG * PTS), BF16)
     parts = ((NG, COLS, PTS), F32)
+    bases = ((NG, PTS, PTS), BF16)
     rows1 = ((COLS + 1, PTS), F32)
-    rows2 = ((COLS + 2, PTS), F32)
     held = pltpu.VMEM((4, COEFS, PTS), F32)
     two = [pltpu.VMEM((COLS, PTS), F32)] * 2
     dma = pltpu.SemaphoreType.DMA
@@ -380,8 +376,8 @@
     got_b = gather(send, GB)
     (send,) = call(fold0_kernel, [((SEND0, PTS), F32)], got_b, send, basis, leaf_part, name="fold0")
     got_a = gather(send, GA)
-    high, low, out, z0, table0 = call(
-        first_kernel, [block, block, parts, vec, table], marks, got_a, got_b, limit=24 << 20,
+    high, low, out, z0, table0, bases_high, bases_low = call(
+        first_kernel, [block, block, parts, vec, table, bases, bases], marks, got_a, got_b, limit=24 << 20,
         scratch=[
             pltpu.VMEM((NG, COLS, PTS), F32), pltpu.VMEM((NG * PTS, PTS), BF16), pltpu.VMEM((PTS, NG * PTS), BF16),
             pltpu.VMEM((NG, 2 * COLS, PTS), BF16),
@@ -392,14 +388,14 @@
     (send,) = call(fold1_kernel, [((COEFS + 1 + COLS, PTS), F32)], gather(send[:, None], GB), leaf_q, scratch=two, name="fold1")
     out, z1, res, leaf_res, table1, table_q, sums0 = call(
         second_kernel, [parts, vec, vec, vec, table, table, ((1, PTS), F32)],
-        marks, gather(send[:, None], GA), got_a, table0, rhs, q, leaf_part, leaf_q, high, low,
+        marks, gather(send[:, None], GA), got_a, bases_high, bases_low, table0, rhs, q, leaf_part, leaf_q, high, low,
         limit=24 << 20,
         scratch=[pltpu.VMEM((NG, COLS, PTS), F32), held, pltpu.VMEM((NG, COLS, PTS), F32)], name="second",
     )
     p, send = call(
-        image1_kernel, [vec, rows2], scatter(out), z1, z0, res, q, leaf_res, leaf_q, leaf, basis, name="image1"
-    )
-    (send,) = call(fold2_kernel, [((COEFS + 2, PTS), F32)], gather(send[:, None], GB), scratch=two, name="fold2")
+        image1_kernel, [vec, rows1], scatter(out), z1, res, q, leaf_res, leaf_q, leaf, basis, name="image1"
+    )
+    (send,) = call(fold2_kernel, [((COEFS + 1, PTS), F32)], gather(send[:, None], GB), scratch=two, name="fold2")
     x_out, r_out, coefs = call(
         finish_kernel, [vec, vec, ((2, 2, COLS), F32)],
         gather(send[:, None], GA), z0, z1, res, q, p, table1, table_q, sums0,

time: 139 us -> 139 us (level)
  no operation moved by 1% of the time
where the time goes in v4:
time: 139 us; the launch traced here: 138 us
  blocking collectives  122 us (88%)
  Pallas kernels  15.3 us (11%)
    all_to_all x6, blocking collectives, gather(): lax.all_to_all(jnp.broadcast_to(block[None], (NG,) + block.shape), axes,...  97.2 us
    all_to_all x2, blocking collectives, scatter(): return lax.all_to_all(parts, GB, 0, 0, tiled=True)  24.7 us
    pallas_call x9, Pallas kernels, call(): pl.pallas_call(kernel, out_shape=[m(s, d) if m is HBM else jax.ShapeDtype...  15.3 us

profile of v4, /device:TPU:1, one launch (start us, length us, event | category | flops | bytes accessed | tf_op | source)
XLA Modules:
  0.0 138.4 jit_solution(1425044146680036359)
XLA Ops:
  0.6 1.3 start.1
  2.0 21.6 %all_to_all.40.got.got_b = f32[16,32,128]{2,1,0:T(8,128)S(1)} all-to-all(f32[16,32,128]{2,1,0:T(8,128)S(1)} %broadcast_in_dim.15), channel_id=1, replica_groups=mesh['zl'=2,'y'=4,'zh'=4,'x'=4,'c'=2] {'zl','zh','c'}, dimensions={0} | all-to-all | bytes 524288 | tf_op jit(solution)/shard_map/all_to_all | solution.py:346
  23.6 0.1 fold0.1
  23.7 0.1 broadcast_in_dim.16
  23.8 29.5 %all_to_all.41.got_a.got0 = f32[16,184,128]{2,1,0:T(8,128)S(1)} all-to-all(f32[16,184,128]{2,1,0:T(8,128)S(1)} %broadcast_in_dim.16), channel_id=1, replica_groups=mesh['zl'=2,'y'=4,'zh'=4,'x'=4,'c'=2] {'y','x'}, dimensions={0} | all-to-all | bytes 3014656 | tf_op jit(solution)/shard_map/all_to_all | solution.py:346
  53.3 9.2 %first.1 = (bf16[2048,2048]{1,0:T(8,128)(2,1)S(1)}, bf16[2048,2048]{1,0:T(8,128)(2,1)S(1)}, f32[16,16,128]{2,1,0:T(8,128)S(1)}, f32[16,128]{1,0:T(8,128)S(1)}, f...) custom-call(f32[24,128]{1,0:T(8,128)S(1)} %get-tuple-element.28.marks, ...), custom_call_target="tpu_custom_call" | custom-call | tf_op jit(solution)/shard_map/first/pallas_call | solution.py:89
  62.5 11.9 %all_to_all.42.got = f32[16,16,128]{2,1,0:T(8,128)S(1)} all-to-all(f32[16,16,128]{2,1,0:T(8,128)S(1)} %get-tuple-element.32), channel_id=1, replica_groups=mesh['zl'=2,'y'=4,'zh'=4,'x'=4,'c'=2] {'zl','zh','c'}, dimensions={0} | all-to-all | bytes 262144 | tf_op jit(solution)/shard_map/all_to_all | solution.py:350
  74.4 0.4 image0.1
  74.8 0.1 broadcast_in_dim.17
  74.9 11.8 %all_to_all.43.got = f32[16,17,1,128]{3,2,1,0:T(1,128)S(1)} all-to-all(f32[16,17,1,128]{3,2,1,0:T(1,128)S(1)} %broadcast_in_dim.17), channel_id=1, replica_groups=mesh['zl'=2,'y'=4,'zh'=4,'x'=4,'c'=2] {'zl','zh','c'}, dimensions={0} | all-to-all | bytes 278528 | tf_op jit(solution)/shard_map/all_to_all | solution.py:346
  86.7 0.1 fold1.1
  86.8 0.2 broadcast_in_dim.18
  87.0 11.9 %all_to_all.44.got = f32[16,41,1,128]{3,2,1,0:T(1,128)S(1)} all-to-all(f32[16,41,1,128]{3,2,1,0:T(1,128)S(1)} %broadcast_in_dim.18), channel_id=1, replica_groups=mesh['zl'=2,'y'=4,'zh'=4,'x'=4,'c'=2] {'y','x'}, dimensions={0} | all-to-all | bytes 671744 | tf_op jit(solution)/shard_map/all_to_all | solution.py:346
  98.9 2.9 %second.1 = (f32[16,16,128]{2,1,0:T(8,128)S(1)}, f32[16,128]{1,0:T(8,128)S(1)}, f32[16,128]{1,0:T(8,128)S(1)}, f32[16,128]{1,0:T(8,128)S(1)}, f32[8,16,128]{2,1,...) custom-call(f32[24,128]{1,0:T(8,128)S(1)} %get-tuple-element.28.marks, ...), custom_call_target="tpu_custom_call" | custom-call | tf_op jit(solution)/shard_map/second/pallas_call | solution.py:89
  101.8 12.8 %all_to_all.45.got = f32[16,16,128]{2,1,0:T(8,128)S(1)} all-to-all(f32[16,16,128]{2,1,0:T(8,128)S(1)} %get-tuple-element.44), channel_id=1, replica_groups=mesh['zl'=2,'y'=4,'zh'=4,'x'=4,'c'=2] {'zl','zh','c'}, dimensions={0} | all-to-all | bytes 262144 | tf_op jit(solution)/shard_map/all_to_all | solution.py:350
  114.5 0.4 image1.1
  114.9 0.1 broadcast_in_dim.19
  115.0 11.8 %all_to_all.46.got = f32[16,17,1,128]{3,2,1,0:T(1,128)S(1)} all-to-all(f32[16,17,1,128]{3,2,1,0:T(1,128)S(1)} %broadcast_in_dim.19), channel_id=1, replica_groups=mesh['zl'=2,'y'=4,'zh'=4,'x'=4,'c'=2] {'zl','zh','c'}, dimensions={0} | all-to-all | bytes 278528 | tf_op jit(solution)/shard_map/all_to_all | solution.py:346
  126.8 0.1 fold2.1
  126.9 0.1 broadcast_in_dim.20
  127.0 10.6 %all_to_all.47.got = f32[16,25,1,128]{3,2,1,0:T(1,128)S(1)} all-to-all(f32[16,25,1,128]{3,2,1,0:T(1,128)S(1)} %broadcast_in_dim.20), channel_id=1, replica_groups=mesh['zl'=2,'y'=4,'zh'=4,'x'=4,'c'=2] {'y','x'}, dimensions={0} | all-to-all | bytes 409600 | tf_op jit(solution)/shard_map/all_to_all | solution.py:346
  137.6 0.8 finish.1
  (1 shorter events, 0.0 us)

commit v5 on v4

--- a/solution.py
+++ b/solution.py
@@ -104,18 +104,18 @@
 LEAF_PART = slice(SEND0 - COLS, SEND0)
 
 
-def start_kernel(where, inv_h, points_h, target_h, bits_h, top_h, sub_h, leaf_h, send, rhs, basis, leaf, leaf_part, marks, points, target, bits, inv, sems):
+def start_kernel(where, inv_h, points_h, target_h, bits_h, top_h, sub_h, leaf_h, send, rhs, weights, leaf_part, marks, points, target, bits, inv, sems):
     moves = [
         pltpu.make_async_copy(src, dst, sems.at[k])
         for k, (src, dst) in enumerate(
             [
                 (bits_h, bits),
                 (target_h, target),
-                (top_h, basis.at[pl.ds(0, RANK)]),
-                (sub_h, basis.at[pl.ds(RANK, RANK)]),
+                (top_h, weights.at[pl.ds(0, RANK)]),
+                (sub_h, weights.at[pl.ds(RANK, RANK)]),
                 (points_h, points),
                 (inv_h, inv),
-                (leaf_h, leaf),
+                (leaf_h, weights.at[pl.ds(PTS, PTS)]),
             ]
         )
     ]
@@ -133,8 +133,9 @@
     rhs[0:1, :] = target[...]
     rhs[1:COLS, :] = 2.0 * bits[...].astype(F32) - 1.0
     send[0:COLS, :] = points[...] * scale
-    send[COLS : 2 * COLS, :] = dot_nt(rhs[...], basis[...])
-    leaf_part[...] = dot_nt(rhs[...], leaf[...])
+    both = dot_nt(rhs[...], weights[...])
+    send[COLS : 2 * COLS, :] = both[:, 0:PTS]
+    leaf_part[...] = both[:, PTS:]
 
 
 def pack_half(tile):
@@ -145,14 +146,14 @@
     return jnp.concatenate([pltpu.roll(packed, RANK, 1), packed], 0)
 
 
-def fold0_kernel(got, own, basis, leaf_part, send):
+def fold0_kernel(got, own, weights, leaf_part, send):
     low = lane((COLS, PTS)) < RANK
     zero = tree_sum([got[j, COLS : 2 * COLS] for j in range(NG // 2)])
     one = tree_sum([got[j, COLS : 2 * COLS] for j in range(NG // 2, NG)])
     send[0:COLS, :] = own[0:COLS, :]
     send[COLS : 2 * COLS, :] = jnp.where(low, zero + one, zero)
     send[2 * COLS : 5 * COLS // 2, :] = pack_half(one)
-    send[BASES, :] = basis[...]
+    send[BASES, :] = weights[0:PTS, :]
     send[LEAF_PART, :] = leaf_part[...]
 
 
@@ -278,10 +279,11 @@
             out[j // PTS + b] = r[:, b * PTS : (b + 1) * PTS]
 
 
-def image0_kernel(got, z, rhs, basis, leaf, q, leaf_part, send):
+def image0_kernel(got, z, rhs, weights, q, leaf_part, send):
     q[...] = tree_sum([got[j] for j in range(NG)]) + NOISE * z[...]
-    leaf_part[...] = dot_nt(q[...], leaf[...])
-    send_rows(send, dot_nt(q[...], basis[...]), [
+    both = dot_nt(q[...], weights[...])
+    leaf_part[...] = both[:, PTS:]
+    send_rows(send, both[:, 0:PTS], [
         pack([rowdot(rhs[...], z[...]), rowdot(z[...], q[...]), rowdot(q[...], leaf_part[...])])
     ])
 
@@ -309,13 +311,14 @@
     matvec(directions, high, low, out)
 
 
-def image1_kernel(got, z1, res, q, leaf_res, leaf_q, leaf, basis, p, send):
+def image1_kernel(got, z1, res, q, leaf_res, leaf_q, weights, p, send):
     p[...] = tree_sum([got[j] for j in range(NG)]) + NOISE * z1[...]
     rv, qv, pv, zv = res[...], q[...], p[...], z1[...]
-    rb, qb, pb = leaf_res[...], leaf_q[...], dot_nt(pv, leaf[...])
+    both = dot_nt(pv, weights[...])
+    rb, qb, pb = leaf_res[...], leaf_q[...], both[:, PTS:]
     pairs = ((rv, zv), (zv, pv), (zv, qv), (rv, rb), (rv, qb), (rv, pb), (qv, pb), (pv, pb))
     rows = [pack([rowdot(a, b) for a, b in pairs])]
-    send_rows(send, dot_nt(pv, basis[...]), rows)
+    send_rows(send, both[:, 0:PTS], rows)
 
 
 def finish_kernel(got, z0, z1, res, q, p, table1, table_q, sums0, x_out, r_out, coefs, held):
@@ -352,7 +355,6 @@
 
 def on_device(points, inverse_length, target, probe_bits, leaf_inverse, top_basis, sub_basis):
     vec = ((COLS, PTS), F32)
-    square = ((PTS, PTS), F32)
     table = ((NT, COLS, PTS), F32)
     block = ((NG * PTS, NG * PTS), BF16)
     parts = ((NG, COLS, PTS), F32)
@@ -362,9 +364,9 @@
     two = [pltpu.VMEM((COLS, PTS), F32)] * 2
     dma = pltpu.SemaphoreType.DMA
     where = lax.axis_index(("zl",) + GA).astype(jnp.int32).reshape(1)
-    send, rhs, basis, leaf, leaf_part, marks = call(
+    send, rhs, weights, leaf_part, marks = call(
         start_kernel,
-        [((2 * COLS, PTS), F32), vec, square, square, vec, ((NG + 8, PTS), F32)],
+        [((2 * COLS, PTS), F32), vec, ((2 * PTS, PTS), F32), vec, ((NG + 8, PTS), F32)],
         where, inverse_length, points, target[None, :], probe_bits, top_basis, sub_basis, leaf_inverse,
         spaces=[SMEM] + [HBM] * 7,
         scratch=[
@@ -374,7 +376,7 @@
         name="start",
     )
     got_b = gather(send, GB)
-    (send,) = call(fold0_kernel, [((SEND0, PTS), F32)], got_b, send, basis, leaf_part, name="fold0")
+    (send,) = call(fold0_kernel, [((SEND0, PTS), F32)], got_b, send, weights, leaf_part, name="fold0")
     got_a = gather(send, GA)
     high, low, out, z0, table0, bases_high, bases_low = call(
         first_kernel, [block, block, parts, vec, table, bases, bases], marks, got_a, got_b, limit=24 << 20,
@@ -384,7 +386,7 @@
         ],
         name="first",
     )
-    q, leaf_q, send = call(image0_kernel, [vec, vec, rows1], scatter(out), z0, rhs, basis, leaf, name="image0")
+    q, leaf_q, send = call(image0_kernel, [vec, vec, rows1], scatter(out), z0, rhs, weights, name="image0")
     (send,) = call(fold1_kernel, [((COEFS + 1 + COLS, PTS), F32)], gather(send[:, None], GB), leaf_q, scratch=two, name="fold1")
     out, z1, res, leaf_res, table1, table_q, sums0 = call(
         second_kernel, [parts, vec, vec, vec, table, table, ((1, PTS), F32)],
@@ -393,7 +395,7 @@
         scratch=[pltpu.VMEM((NG, COLS, PTS), F32), held, pltpu.VMEM((NG, COLS, PTS), F32)], name="second",
     )
     p, send = call(
-        image1_kernel, [vec, rows1], scatter(out), z1, res, q, leaf_res, leaf_q, leaf, basis, name="image1"
+        image1_kernel, [vec, rows1], scatter(out), z1, res, q, leaf_res, leaf_q, weights, name="image1"
     )
     (send,) = call(fold2_kernel, [((COEFS + 1, PTS), F32)], gather(send[:, None], GB), scratch=two, name="fold2")
     x_out, r_out, coefs = call(

time: 139 us -> 139 us (level)
  no operation moved by 1% of the time
where the time goes in v5:
time: 139 us; the launch traced here: 138 us
  blocking collectives  122 us (88%)
  Pallas kernels  15 us (11%)
    all_to_all x6, blocking collectives, gather(): lax.all_to_all(jnp.broadcast_to(block[None], (NG,) + block.shape), axes,...  97.2 us
    all_to_all x2, blocking collectives, scatter(): return lax.all_to_all(parts, GB, 0, 0, tiled=True)  24.7 us
    pallas_call x9, Pallas kernels, call(): pl.pallas_call(kernel, out_shape=[m(s, d) if m is HBM else jax.ShapeDtype...  15 us

profile of v5, /device:TPU:1, one launch (start us, length us, event | category | flops | bytes accessed | tf_op | source)
XLA Modules:
  0.0 138.1 jit_solution(1959194165930006972)
XLA Ops:
  0.6 1.2 start.1
  1.9 21.6 %all_to_all.40.got.got_b = f32[16,32,128]{2,1,0:T(8,128)S(1)} all-to-all(f32[16,32,128]{2,1,0:T(8,128)S(1)} %broadcast_in_dim.15), channel_id=1, replica_groups=mesh['zl'=2,'y'=4,'zh'=4,'x'=4,'c'=2] {'zl','zh','c'}, dimensions={0} | all-to-all | bytes 524288 | tf_op jit(solution)/shard_map/all_to_all | solution.py:349
  23.5 0.1 fold0.1
  23.6 0.1 broadcast_in_dim.16
  23.7 29.5 %all_to_all.41.got_a.got0 = f32[16,184,128]{2,1,0:T(8,128)S(1)} all-to-all(f32[16,184,128]{2,1,0:T(8,128)S(1)} %broadcast_in_dim.16), channel_id=1, replica_groups=mesh['zl'=2,'y'=4,'zh'=4,'x'=4,'c'=2] {'y','x'}, dimensions={0} | all-to-all | bytes 3014656 | tf_op jit(solution)/shard_map/all_to_all | solution.py:349
  53.2 9.2 %first.1 = (bf16[2048,2048]{1,0:T(8,128)(2,1)S(1)}, bf16[2048,2048]{1,0:T(8,128)(2,1)S(1)}, f32[16,16,128]{2,1,0:T(8,128)S(1)}, f32[16,128]{1,0:T(8,128)S(1)}, f...) custom-call(f32[24,128]{1,0:T(8,128)S(1)} %get-tuple-element.27.marks, ...), custom_call_target="tpu_custom_call" | custom-call | tf_op jit(solution)/shard_map/first/pallas_call | solution.py:89
  62.4 11.9 %all_to_all.42.got = f32[16,16,128]{2,1,0:T(8,128)S(1)} all-to-all(f32[16,16,128]{2,1,0:T(8,128)S(1)} %get-tuple-element.31), channel_id=1, replica_groups=mesh['zl'=2,'y'=4,'zh'=4,'x'=4,'c'=2] {'zl','zh','c'}, dimensions={0} | all-to-all | bytes 262144 | tf_op jit(solution)/shard_map/all_to_all | solution.py:353
  74.3 0.3 image0.1
  74.6 0.1 broadcast_in_dim.17
  74.7 11.8 %all_to_all.43.got = f32[16,17,1,128]{3,2,1,0:T(1,128)S(1)} all-to-all(f32[16,17,1,128]{3,2,1,0:T(1,128)S(1)} %broadcast_in_dim.17), channel_id=1, replica_groups=mesh['zl'=2,'y'=4,'zh'=4,'x'=4,'c'=2] {'zl','zh','c'}, dimensions={0} | all-to-all | bytes 278528 | tf_op jit(solution)/shard_map/all_to_all | solution.py:349
  86.5 0.1 fold1.1
  86.6 0.2 broadcast_in_dim.18
  86.8 11.9 %all_to_all.44.got = f32[16,41,1,128]{3,2,1,0:T(1,128)S(1)} all-to-all(f32[16,41,1,128]{3,2,1,0:T(1,128)S(1)} %broadcast_in_dim.18), channel_id=1, replica_groups=mesh['zl'=2,'y'=4,'zh'=4,'x'=4,'c'=2] {'y','x'}, dimensions={0} | all-to-all | bytes 671744 | tf_op jit(solution)/shard_map/all_to_all | solution.py:349
  98.7 2.9 %second.1 = (f32[16,16,128]{2,1,0:T(8,128)S(1)}, f32[16,128]{1,0:T(8,128)S(1)}, f32[16,128]{1,0:T(8,128)S(1)}, f32[16,128]{1,0:T(8,128)S(1)}, f32[8,16,128]{2,1,...) custom-call(f32[24,128]{1,0:T(8,128)S(1)} %get-tuple-element.27.marks, ...), custom_call_target="tpu_custom_call" | custom-call | tf_op jit(solution)/shard_map/second/pallas_call | solution.py:89
  101.6 12.8 %all_to_all.45.got = f32[16,16,128]{2,1,0:T(8,128)S(1)} all-to-all(f32[16,16,128]{2,1,0:T(8,128)S(1)} %get-tuple-element.42), channel_id=1, replica_groups=mesh['zl'=2,'y'=4,'zh'=4,'x'=4,'c'=2] {'zl','zh','c'}, dimensions={0} | all-to-all | bytes 262144 | tf_op jit(solution)/shard_map/all_to_all | solution.py:353
  114.3 0.3 image1.1
  114.6 0.1 broadcast_in_dim.19
  114.7 11.8 %all_to_all.46.got = f32[16,17,1,128]{3,2,1,0:T(1,128)S(1)} all-to-all(f32[16,17,1,128]{3,2,1,0:T(1,128)S(1)} %broadcast_in_dim.19), channel_id=1, replica_groups=mesh['zl'=2,'y'=4,'zh'=4,'x'=4,'c'=2] {'zl','zh','c'}, dimensions={0} | all-to-all | bytes 278528 | tf_op jit(solution)/shard_map/all_to_all | solution.py:349
  126.5 0.1 fold2.1
  126.6 0.1 broadcast_in_dim.20
  126.7 10.6 %all_to_all.47.got = f32[16,25,1,128]{3,2,1,0:T(1,128)S(1)} all-to-all(f32[16,25,1,128]{3,2,1,0:T(1,128)S(1)} %broadcast_in_dim.20), channel_id=1, replica_groups=mesh['zl'=2,'y'=4,'zh'=4,'x'=4,'c'=2] {'y','x'}, dimensions={0} | all-to-all | bytes 409600 | tf_op jit(solution)/shard_map/all_to_all | solution.py:349
  137.3 0.8 finish.1
  (1 shorter events, 0.0 us)
